TPU v7x, 32 devices: a whole 2x2x4 slice. The times are simulated.
32 devices in a mesh: groups: 2 (over x), along: 8 (over z, y), across: 2 (over core).
Axes of the slice: x: 2, y: 2, z: 4, core: 2. Of those that a mesh axis runs over, the one named last changes fastest.
Arguments:
- toa_bands: bfloat16 [1024, 4, 2048], P(('groups', 'along'), None, 'across'), parts along dimension 0, may hold values from 0.019897461 to 0.59765625
- dark_mask: int32 [1024, 2048], P(('groups', 'along'), 'across'), parts along dimension 0, may hold values 0 or 1
- vapour: float32 [1024, 2048], P(('groups', 'along'), 'across'), parts along dimension 0, may hold values from 0 to 7
- elev_class: int32 [1024, 2048], P(('groups', 'along'), 'across'), parts along dimension 0, may hold values from 0 to 6
- elev_frac: float32 [1024, 2048], P(('groups', 'along'), 'across'), parts along dimension 0, may hold values from 0 to 1
- kernel: float32 [61], replicated, may hold values from 0.1 to 1
- lut_gain: bfloat16 [4, 8, 16, 8], replicated, may hold values from 1 to 2
- lut_path: bfloat16 [4, 8, 16, 8], replicated, may hold values from 0 to 0.29882812
- lut_albedo: bfloat16 [4, 8, 16, 8], replicated, may hold values from 0.049804688 to 0.25
- routes: int32 [64, 2], P(('groups', 'along')), parts along dimension 0, may hold values from 0 to 7, as said below
- starts: int32 [64, 2], P(('groups', 'along')), parts along dimension 0, may hold values from 0 to 48
Outputs:
- tile_out: bfloat16 [16, 64, 4, 2048], P(('groups', 'along'), None, None, 'across'), parts along dimension 0
There are 2 independent parts, one for each index of `groups`. A program takes and returns all parts, laid end to end along the dimension named above; an argument that names none is the same for every part. Nothing has to cross between parts.
Inputs may be any that keep to these rules, and one draw needn't show every extreme that they name: `dark_mask`: 1 marks a dark pixel. `elev_class`: the class and the next one are both classes of the table. `routes`: the first block of segment s is s // 4, the block of the segment's own rows; the second lies 1 to 2 blocks before or after it; among the 4 segments of one device at most 2 have their second block at any one signed distance, and in every draw some device has exactly 2 at some distance.
All inputs are finite; a program needn't handle non-finite values. No bound on the sum of `dark_mask` on one device may be relied on, other than what follows from the above.
Results may differ from a plain program's by a relative error of at most 0.0043.
Values may be sent and summed in bfloat16 or wider, within the bound.
A program may use at most 64 MiB of HBM per device.

v0:
```python
import math

import jax
import jax.numpy as jnp
from jax import lax
from jax.sharding import PartitionSpec as P

SEG = 16
REACH = 2
CAP = 2


highest = lax.Precision.HIGHEST


def with_halo(block, sides, width):
    for axis, dim in sides:
        count = lax.axis_size(axis)
        forward = [(i, i + 1) for i in range(count - 1)]
        backward = [(target, source) for source, target in forward]
        low = lax.ppermute(
            lax.slice_in_dim(block, block.shape[dim] - width, None, axis=dim), axis, forward
        )
        high = lax.ppermute(lax.slice_in_dim(block, 0, width, axis=dim), axis, backward)
        block = jnp.concatenate([low, block, high], axis=dim)
    return block


def from_behind(value, axis, steps):
    count = lax.axis_size(axis)
    initial, last = (max(0, -steps), min(count, count - steps))
    return lax.ppermute(value, axis, [(source, source + steps) for source in range(initial, last)])


def band_matrix(kernel, block_size):
    tap_count = kernel.shape[0]
    rows_at = jnp.arange(block_size + tap_count - 1)[:, None, None]
    cols_at = jnp.arange(block_size)[None, :, None]
    tap_ids = jnp.arange(tap_count)[None, None, :]
    return jnp.sum(jnp.where(rows_at - cols_at == tap_ids, kernel[None, None, :], 0.0), axis=2)


def smooth_rows(fields, kernel):
    tap_count = kernel.shape[0]
    length = fields.shape[1] - tap_count + 1
    block_size = math.gcd(length, 128)
    matrix = band_matrix(kernel, block_size)
    pieces = jnp.einsum("mr,fmc->frc", matrix, fields, precision=highest)
    return pieces


def smooth_cols(fields, kernel):
    tap_count = kernel.shape[0]
    length = fields.shape[2] - tap_count + 1
    block_size = math.gcd(length, 128)
    matrix = band_matrix(kernel, block_size)
    pieces = []
    for number in range(length // block_size):
        window = fields[
            :, :, number * block_size : number * block_size + block_size + tap_count - 1
        ]
        pieces.append(jnp.einsum("frm,mc->frc", window, matrix, precision=highest))
    return jnp.concatenate(pieces, axis=2)


def place_rows(rows, first, tile_rows):
    placed = (
        jnp.arange(tile_rows)[None, :, None]
        == first[:, None, None] + jnp.arange(SEG)[None, None, :]
    ) & (first >= 0)[:, None, None]
    summed = jnp.einsum(
        "srj,sjx->rx", placed.astype(jnp.bfloat16), rows, preferred_element_type=jnp.float32
    )
    counts = jnp.sum(placed.astype(jnp.float32), axis=(0, 2))
    return (summed, counts)


def body(
    toa_bands,
    dark_mask,
    vapour,
    elev_class,
    elev_frac,
    kernel,
    lut_gain,
    lut_path,
    lut_albedo,
    routes,
    starts,
):
    row_count, band_count, col_count = toa_bands.shape
    half_width = kernel.shape[0] // 2
    levels_e, levels_a, levels_w = (lut_gain.shape[1], lut_gain.shape[2], lut_gain.shape[3])
    darkness = dark_mask.astype(jnp.float32)
    blue_band = toa_bands[:, 0, :].astype(jnp.float32)
    red_band = toa_bands[:, 2, :].astype(jnp.float32)
    fields = jnp.stack([darkness * 8.0 * (blue_band - 0.5 * red_band), darkness])
    padded = with_halo(fields, (("along", 1), ("across", 2)), half_width)
    rowwise = smooth_rows(padded, kernel)
    smoothed = smooth_cols(rowwise, kernel)
    aerosol = smoothed[0] / jnp.maximum(smoothed[1], 1.0)
    aero_pos = (levels_a - 1) * jax.nn.sigmoid(aerosol)
    lut_table = jnp.stack([lut_gain, lut_path, lut_albedo], axis=1).reshape(
        band_count * 3 * levels_e, levels_a * levels_w
    )
    block_rows = math.gcd(row_count, 16)
    block_count = row_count // block_rows

    def correct_block(inputs):
        toa_block, pos_block, vapour_block, class_block, frac_block = inputs
        weight_a = jnp.maximum(
            0.0,
            1.0 - jnp.abs(pos_block[None] - jnp.arange(levels_a, dtype=jnp.float32)[:, None, None]),
        )
        weight_w = jnp.maximum(
            0.0,
            1.0
            - jnp.abs(vapour_block[None] - jnp.arange(levels_w, dtype=jnp.float32)[:, None, None]),
        )
        joint_weight = (
            (weight_a[:, None] * weight_w[None])
            .reshape(levels_a * levels_w, block_rows * col_count)
            .astype(jnp.bfloat16)
        )
        node_values = jnp.dot(lut_table, joint_weight, preferred_element_type=jnp.float32)
        node_values = node_values.reshape(band_count, 3, levels_e, block_rows, col_count)
        elev_ids = jnp.arange(levels_e)[:, None, None]
        weight_e = jnp.where(elev_ids == class_block[None], 1.0 - frac_block[None], 0.0)
        weight_e = weight_e + jnp.where(elev_ids == class_block[None] + 1, frac_block[None], 0.0)
        coefficient = jnp.sum(node_values * weight_e[None, None], axis=2)
        radiance = jnp.transpose(toa_block.astype(jnp.float32), (1, 0, 2))
        scaled = coefficient[:, 0] * radiance - coefficient[:, 1]
        surface = scaled / (1.0 + coefficient[:, 2] * scaled)
        return jnp.transpose(surface, (1, 0, 2)).astype(jnp.bfloat16)

    inputs = (
        toa_bands.reshape(block_count, block_rows, band_count, col_count),
        aero_pos.reshape(block_count, block_rows, col_count),
        vapour.reshape(block_count, block_rows, col_count),
        elev_class.reshape(block_count, block_rows, col_count),
        elev_frac.reshape(block_count, block_rows, col_count),
    )
    corrected = lax.map(correct_block, inputs).reshape(row_count, band_count, col_count)
    seg_dev = routes.shape[0]
    row_width = band_count * col_count
    own_tile = lax.axis_index("along")
    segment_rows = corrected.reshape(seg_dev, SEG, row_width)
    own_first = jnp.where(routes[:, 0] == own_tile, starts[:, 0], -1)
    summed, counts = place_rows(segment_rows, own_first, row_count)
    sides = [side - REACH for side in range(REACH)] + [side + 1 for side in range(REACH)]
    flat_rows = segment_rows.reshape(seg_dev, SEG * row_width)
    distance = routes[:, 1] - own_tile
    for side in sides:
        is_side = (distance == side).astype(jnp.int32)
        rank = jnp.cumsum(is_side) - is_side
        chosen = (is_side[None, :] == 1) & (rank[None, :] == jnp.arange(CAP)[:, None])
        outgoing = jnp.dot(
            chosen.astype(jnp.bfloat16), flat_rows, preferred_element_type=jnp.float32
        ).astype(jnp.bfloat16)
        slot_tag = jnp.sum(jnp.where(chosen, starts[:, 1][None, :] + 1, 0), axis=1)
        got_rows, got_tag = from_behind((outgoing, slot_tag), "along", side)
        part_sum, part_count = place_rows(
            got_rows.reshape(CAP, SEG, row_width), got_tag - 1, row_count
        )
        summed = summed + part_sum
        counts = counts + part_count
    tile_out = (summed / jnp.maximum(counts, 1.0)[:, None]).astype(jnp.bfloat16)
    return tile_out.reshape(1, row_count, band_count, col_count)


def solution(mesh):
    in_specs = (
        P(("groups", "along"), None, "across"),
        P(("groups", "along"), "across"),
        P(("groups", "along"), "across"),
        P(("groups", "along"), "across"),
        P(("groups", "along"), "across"),
        P(),
        P(),
        P(),
        P(),
        P(("groups", "along"), None),
        P(("groups", "along"), None),
    )
    out_specs = P(("groups", "along"), None, None, "across")
    return jax.shard_map(body, mesh=mesh, in_specs=in_specs, out_specs=out_specs, check_vma=False)
```

profile of v0, /device:TPU:0, one launch (start us, length us, event | category | flops | bytes accessed | tf_op | source)
XLA Modules:
  0.0 118.5 jit_solution(6398646044948553667)
XLA Ops:
  0.0 1.1 copy.51
  1.2 1.7 %fusion.77 = (bf16[64,1,1024]{2,1,0:T(2,128)(2,1)S(1)}, bf16[64,1,1024]{2,1,0:T(2,128)(2,1)S(1)}) fusion(bf16[64,4,1024]{2,1,0:T(4,128)(2,1)} %param.13), kind=kLoop, calls=%fused_computation.170 | loop fusion | bytes 524288 | tf_op jit(solution)/shard_map/slice | solution.py:95
  3.8 1.0 copy.55
  4.9 1.3 %collective-permute-start.1 = (f32[2,30,1024]{2,0,1:T(2,128)}, f32[2,30,1024]{2,0,1:T(2,128)}, u32[]{:S(2)}, u32[]{:S(2)}) collective-permute-start(f32[2,30,1024]{2,0,1:T(2,128)} %copy.55), channel_id=1, source_target_pairs={{2,0},{4,2},{6,4},{8,6},{10,8},{12,10},{14,12},{3,1},{5,3},{7,5},{... | collective-permute-start | bytes 737288 | tf_op jit(solution)/shard_map/ppermute | solution.py:24
  6.2 1.0 copy.54
  7.2 5.5 %collective-permute-start = (f32[2,30,1024]{2,0,1:T(2,128)}, f32[2,30,1024]{2,0,1:T(2,128)S(1)}, u32[]{:S(2)}, u32[]{:S(2)}) collective-permute-start(f32[2,30,1024]{2,0,1:T(2,128)} %copy.54), channel_id=1, source_target_pairs={{0,2},{2,4},{4,6},{6,8},{8,10},{10,12},{12,14},{1,3},{3,5},{5,7},{... | collective-permute-start | bytes 737288 | tf_op jit(solution)/shard_map/ppermute | solution.py:21
  13.6 4.0 %collective-permute-start.10 = (s32[2]{0:T(128)S(1)}, s32[2]{0:T(128)S(1)}, u32[]{:S(2)}, u32[]{:S(2)}) collective-permute-start(s32[2]{0:T(128)S(1)} %get-tuple-element.67), channel_id=1, source_target_pairs={{0,4},{2,6},{4,8},{6,10},{8,12},{10,14},{1,5},{3,7},{5,9},{7,11},{... | collective-permute-start | bytes 32 | tf_op jit(solution)/shard_map/ppermute | solution.py:32
  17.6 4.3 %collective-permute-start.8 = (s32[2]{0:T(128)S(1)}, s32[2]{0:T(128)S(1)}, u32[]{:S(2)}, u32[]{:S(2)}) collective-permute-start(s32[2]{0:T(128)S(1)} %get-tuple-element.66), channel_id=1, source_target_pairs={{0,2},{2,4},{4,6},{6,8},{8,10},{10,12},{12,14},{1,3},{3,5},{5,7},{... | collective-permute-start | bytes 32 | tf_op jit(solution)/shard_map/ppermute | solution.py:32
  21.9 1.3 %collective-permute-start.6 = (s32[2]{0:T(128)S(1)}, s32[2]{0:T(128)S(1)}, u32[]{:S(2)}, u32[]{:S(2)}) collective-permute-start(s32[2]{0:T(128)S(1)} %get-tuple-element.65), channel_id=1, source_target_pairs={{2,0},{4,2},{6,4},{8,6},{10,8},{12,10},{14,12},{3,1},{5,3},{7,5},{... | collective-permute-start | bytes 32 | tf_op jit(solution)/shard_map/ppermute | solution.py:32
  25.2 1.3 %collective-permute-start.4 = (s32[2]{0:T(128)S(1)}, s32[2]{0:T(128)S(1)}, u32[]{:S(2)}, u32[]{:S(2)}) collective-permute-start(s32[2]{0:T(128)S(1)} %get-tuple-element.64), channel_id=1, source_target_pairs={{4,0},{6,2},{8,4},{10,6},{12,8},{14,10},{5,1},{7,3},{9,5},{11,7},{... | collective-permute-start | bytes 32 | tf_op jit(solution)/shard_map/ppermute | solution.py:32
  27.5 3.9 %collective-permute-done.4 = s32[2]{0:T(128)S(1)} collective-permute-done((s32[2]{0:T(128)S(1)}, s32[2]{0:T(128)S(1)}, u32[]{:S(2)}, u32[]{:S(2)}) %collective-permute-start.4) | collective-permute-done | bytes 40 | tf_op jit(solution)/shard_map/ppermute | solution.py:32
  31.9 1.3 %copy.57 = f32[2,30,1024]{1,2,0:T(8,128)S(1)} copy(f32[2,30,1024]{2,0,1:T(2,128)} %collective-permute-done.1) | data formatting | bytes 491520 | tf_op jit(solution)/shard_map/ppermute | solution.py:24
  33.2 1.4 %copy.56 = f32[2,30,1024]{1,2,0:T(8,128)} copy(f32[2,30,1024]{2,0,1:T(2,128)S(1)} %collective-permute-done) | data formatting | bytes 491520 | tf_op jit(solution)/shard_map/ppermute | solution.py:21
  34.6 1.8 %pad_maximum_fusion.1 = f32[2,124,1024]{1,2,0:T(8,128)S(1)} fusion(f32[2,30,1024]{1,2,0:T(8,128)S(1)} %copy.57, f32[1,64,1024]{1,2,0:T(8,128)S(1)} %convert_bitcast_fusion.1, f32[1,64,1024]{1,2,0:T(8,128)S(1)} %fusion.14, f32[2,30,1024]{1,2,0:T(8,128)} %copy.56), kind=kLoop, calls=%fused_computation.58 | loop fusion | flops 761856 | bytes 2031616 | tf_op jit(solution)/shard_map/concatenate | solution.py:25
  36.4 1.4 %collective-permute-start.2 = (f32[2,124,30]{1,2,0:T(8,128)S(1)}, f32[2,124,30]{1,2,0:T(8,128)S(1)}, u32[]{:S(2)}, u32[]{:S(2)}) collective-permute-start(f32[2,124,30]{1,2,0:T(8,128)S(1)} %get-tuple-element.94), channel_id=1, source_target_pairs={{0,1},{2,3},{4,5},{6,7},{8,9},{10,11},{12,13},{14,15},{16,17},{18,... | collective-permute-start | bytes 89288 | tf_op jit(solution)/shard_map/ppermute | solution.py:21
  37.9 1.5 %collective-permute-start.3 = (f32[2,124,30]{1,2,0:T(8,128)S(1)}, f32[2,124,30]{1,2,0:T(8,128)S(1)}, u32[]{:S(2)}, u32[]{:S(2)}) collective-permute-start(f32[2,124,30]{1,2,0:T(8,128)S(1)} %get-tuple-element.93), channel_id=1, source_target_pairs={{1,0},{3,2},{5,4},{7,6},{9,8},{11,10},{13,12},{15,14},{17,16},{19,... | collective-permute-start | bytes 89288 | tf_op jit(solution)/shard_map/ppermute | solution.py:24
  39.4 1.6 %collective-permute-done.3 = f32[2,124,30]{1,2,0:T(8,128)S(1)} collective-permute-done((f32[2,124,30]{1,2,0:T(8,128)S(1)}, f32[2,124,30]{1,2,0:T(8,128)S(1)}, u32[]{:S(2)}, u32[]{:S(2)}) %collective-permute-start.3) | collective-permute-done | bytes 29792 | tf_op jit(solution)/shard_map/ppermute | solution.py:24
  41.0 1.5 %concatenate.10 = f32[2,124,1084]{1,2,0:T(8,128)S(1)} concatenate(f32[2,124,30]{1,2,0:T(8,128)S(1)} %collective-permute-done.2, f32[2,124,1024]{1,2,0:T(8,128)S(1)} %pad_maximum_fusion.1, f32[2,124,30]{1,2,0:T(8,128)S(1)} %collective-permute-done.3), dimensions={2} | concatenate | bytes 2150656 | tf_op jit(solution)/shard_map/concatenate | solution.py:25
  42.5 1.4 %convolution_bitcast_fusion.5 = f32[2,64,1084]{2,1,0:T(8,128)S(1)} fusion(f32[2,124,1084]{1,2,0:T(8,128)S(1)} %concatenate.10, f32[124,64]{0,1:T(8,128)S(1)} %select_reduce_fusion.1), kind=kOutput, calls=%fused_computation.45 | convolution fusion | flops 206462976 | bytes 1662080 | tf_op jit(solution)/shard_map/mr,fmc->frc/dot_general | solution.py:48
  46.2 44.1 %while.10 = (s32[]{:T(128)}, bf16[4,16,4,1024]{3,2,1,0:T(4,128)(2,1)S(1)}, f32[4,16,1024]{2,1,0:T(8,128)S(1)}, f32[4,16,1024]{2,1,0:T(8,128)}, bf16[96,128]{1,0:...) while((s32[]{:T(128)}, ...), condition=%wide.region_4.5_spmd, body=%wide.region_2.4_spmd.sunk | while | flops 412516352 | bytes 38035576 | solution.py:143
  46.2 0.9 subtract_bitcast_fusion.6
  47.7 1.1 fusion.94
  48.8 2.8 %copy.106 = bf16[16,8,16,1024]{3,1,2,0:T(8,128)(2,1)S(1)} copy(bf16[16,8,16,1024]{3,2,1,0:T(8,128)(2,1)S(1)} %fusion.94) | data formatting | bytes 8388608 | tf_op jit(solution)/shard_map/while
  51.6 1.0 fusion.95
  53.6 2.4 %multiply_reduce_fusion.2 = f32[4,3,16,1024]{3,2,1,0:T(8,128)S(1)} fusion(f32[4,3,8,16,1024]{4,2,3,1,0:T(8,128)S(1)} %bitcast.209, f32[8,16,1024]{2,0,1:T(8,128)S(1)} %select_add_fusion.2), kind=kLoop, calls=%fused_computation.1.clone.1 | loop fusion | flops 2949120 | bytes 7602176 | tf_op jit(solution)/shard_map/while/body/eval_jaxpr/reduce_sum | solution.py:130
  56.0 1.0 constant_dynamic-slice_fusion.2
  58.7 1.1 fusion.94
  59.8 2.8 %copy.106 = bf16[16,8,16,1024]{3,1,2,0:T(8,128)(2,1)S(1)} copy(bf16[16,8,16,1024]{3,2,1,0:T(8,128)(2,1)S(1)} %fusion.94) | data formatting | bytes 8388608 | tf_op jit(solution)/shard_map/while
  62.6 1.0 fusion.95
  64.6 2.4 %multiply_reduce_fusion.2 = f32[4,3,16,1024]{3,2,1,0:T(8,128)S(1)} fusion(f32[4,3,8,16,1024]{4,2,3,1,0:T(8,128)S(1)} %bitcast.209, f32[8,16,1024]{2,0,1:T(8,128)S(1)} %select_add_fusion.2), kind=kLoop, calls=%fused_computation.1.clone.1 | loop fusion | flops 2949120 | bytes 7602176 | tf_op jit(solution)/shard_map/while/body/eval_jaxpr/reduce_sum | solution.py:130
  67.0 1.0 constant_dynamic-slice_fusion.2
  69.7 1.1 fusion.94
  70.8 2.8 %copy.106 = bf16[16,8,16,1024]{3,1,2,0:T(8,128)(2,1)S(1)} copy(bf16[16,8,16,1024]{3,2,1,0:T(8,128)(2,1)S(1)} %fusion.94) | data formatting | bytes 8388608 | tf_op jit(solution)/shard_map/while
  73.5 1.0 fusion.95
  75.5 2.4 %multiply_reduce_fusion.2 = f32[4,3,16,1024]{3,2,1,0:T(8,128)S(1)} fusion(f32[4,3,8,16,1024]{4,2,3,1,0:T(8,128)S(1)} %bitcast.209, f32[8,16,1024]{2,0,1:T(8,128)S(1)} %select_add_fusion.2), kind=kLoop, calls=%fused_computation.1.clone.1 | loop fusion | flops 2949120 | bytes 7602176 | tf_op jit(solution)/shard_map/while/body/eval_jaxpr/reduce_sum | solution.py:130
  78.0 1.0 constant_dynamic-slice_fusion.2
  80.7 1.1 fusion.94
  81.8 2.8 %copy.106 = bf16[16,8,16,1024]{3,1,2,0:T(8,128)(2,1)S(1)} copy(bf16[16,8,16,1024]{3,2,1,0:T(8,128)(2,1)S(1)} %fusion.94) | data formatting | bytes 8388608 | tf_op jit(solution)/shard_map/while
  84.5 1.0 fusion.95
  86.5 2.4 %multiply_reduce_fusion.2 = f32[4,3,16,1024]{3,2,1,0:T(8,128)S(1)} fusion(f32[4,3,8,16,1024]{4,2,3,1,0:T(8,128)S(1)} %bitcast.209, f32[8,16,1024]{2,0,1:T(8,128)S(1)} %select_add_fusion.2), kind=kLoop, calls=%fused_computation.1.clone.1 | loop fusion | flops 2949120 | bytes 7602176 | tf_op jit(solution)/shard_map/while/body/eval_jaxpr/reduce_sum | solution.py:130
  88.9 1.0 constant_dynamic-slice_fusion.2
  92.5 4.2 %collective-permute-start.11 = (bf16[2,65536]{1,0:T(2,128)(2,1)S(1)}, bf16[2,65536]{1,0:T(2,128)(2,1)S(1)}, u32[]{:S(2)}, u32[]{:S(2)}) collective-permute-start(bf16[2,65536]{1,0:T(2,128)(2,1)S(1)} %convolution_convert_fusion), channel_id=1, source_target_pairs={{0,4},{2,6},{4,8},{6,10},{8,12},{10,14},{1,5},{3,7},{5,9},{7,11},{... | collective-permute-start | bytes 786440 | tf_op jit(solution)/shard_map/ppermute | solution.py:32
  96.7 3.2 %collective-permute-start.9 = (bf16[2,65536]{1,0:T(2,128)(2,1)S(1)}, bf16[2,65536]{1,0:T(2,128)(2,1)S(1)}, u32[]{:S(2)}, u32[]{:S(2)}) collective-permute-start(bf16[2,65536]{1,0:T(2,128)(2,1)S(1)} %convolution_convert_fusion.1), channel_id=1, source_target_pairs={{0,2},{2,4},{4,6},{6,8},{8,10},{10,12},{12,14},{1,3},{3,5},{5,7},{... | collective-permute-start | bytes 786440 | tf_op jit(solution)/shard_map/ppermute | solution.py:32
  99.9 1.3 %collective-permute-start.7 = (bf16[2,65536]{1,0:T(2,128)(2,1)S(1)}, bf16[2,65536]{1,0:T(2,128)(2,1)S(1)}, u32[]{:S(2)}, u32[]{:S(2)}) collective-permute-start(bf16[2,65536]{1,0:T(2,128)(2,1)S(1)} %convolution_convert_fusion.2), channel_id=1, source_target_pairs={{2,0},{4,2},{6,4},{8,6},{10,8},{12,10},{14,12},{3,1},{5,3},{7,5},{... | collective-permute-start | bytes 786440 | tf_op jit(solution)/shard_map/ppermute | solution.py:32
  102.0 1.3 %collective-permute-start.5 = (bf16[2,65536]{1,0:T(2,128)(2,1)S(1)}, bf16[2,65536]{1,0:T(2,128)(2,1)S(1)}, u32[]{:S(2)}, u32[]{:S(2)}) collective-permute-start(bf16[2,65536]{1,0:T(2,128)(2,1)S(1)} %convolution_convert_fusion.3), channel_id=1, source_target_pairs={{4,0},{6,2},{8,4},{10,6},{12,8},{14,10},{5,1},{7,3},{9,5},{11,7},{... | collective-permute-start | bytes 786440 | tf_op jit(solution)/shard_map/ppermute | solution.py:32
  103.8 6.7 %collective-permute-done.9 = bf16[2,65536]{1,0:T(2,128)(2,1)S(1)} collective-permute-done((bf16[2,65536]{1,0:T(2,128)(2,1)S(1)}, bf16[2,65536]{1,0:T(2,128)(2,1)S(1)}, u32[]{:S(2)}, u32[]{:S(2)}) %collective-permute-start.9) | collective-permute-done | bytes 262176 | tf_op jit(solution)/shard_map/ppermute | solution.py:32
  111.3 5.6 %collective-permute-done.5 = bf16[2,65536]{1,0:T(2,128)(2,1)S(1)} collective-permute-done((bf16[2,65536]{1,0:T(2,128)(2,1)S(1)}, bf16[2,65536]{1,0:T(2,128)(2,1)S(1)}, u32[]{:S(2)}, u32[]{:S(2)}) %collective-permute-start.5) | collective-permute-done | bytes 262176 | tf_op jit(solution)/shard_map/ppermute | solution.py:32
  117.4 1.2 reshape.420
  (119 shorter events, 22.0 us)
Async XLA Ops:
  2.9 9.9 %copy-start.5 = (s32[4,2]{0,1:T(2,128)S(1)}, s32[4,2]{0,1:T(2,128)}, u32[]{:S(2)}) copy-start(s32[4,2]{0,1:T(2,128)} %param.22) | copy-start | bytes 100
  2.9 10.6 %copy-start.6 = (s32[4,2]{0,1:T(2,128)S(1)}, s32[4,2]{0,1:T(2,128)}, u32[]{:S(2)}) copy-start(s32[4,2]{0,1:T(2,128)} %param.23) | copy-start | bytes 100
  2.9 20.4 %copy-start.4 = (f32[61]{0:T(128)S(1)}, f32[61]{0:T(128)}, u32[]{:S(2)}) copy-start(f32[61]{0:T(128)} %param.18) | copy-start | bytes 736
  3.1 21.2 %copy-start.1 = (bf16[4,8,16,8]{2,3,1,0:T(8,128)(2,1)S(1)}, bf16[4,8,16,8]{2,3,1,0:T(8,128)(2,1)}, u32[]{:S(2)}) copy-start(bf16[4,8,16,8]{2,3,1,0:T(8,128)(2,1)} %param.21) | copy-start | bytes 24580
  3.1 21.2 %copy-start.2 = (bf16[4,8,16,8]{2,3,1,0:T(8,128)(2,1)S(1)}, bf16[4,8,16,8]{2,3,1,0:T(8,128)(2,1)}, u32[]{:S(2)}) copy-start(bf16[4,8,16,8]{2,3,1,0:T(8,128)(2,1)} %param.20) | copy-start | bytes 24580
  3.1 21.2 %copy-start.3 = (bf16[4,8,16,8]{2,3,1,0:T(8,128)(2,1)S(1)}, bf16[4,8,16,8]{2,3,1,0:T(8,128)(2,1)}, u32[]{:S(2)}) copy-start(bf16[4,8,16,8]{2,3,1,0:T(8,128)(2,1)} %param.19) | copy-start | bytes 24580
  4.9 27.0 %collective-permute-start.1 = (f32[2,30,1024]{2,0,1:T(2,128)}, f32[2,30,1024]{2,0,1:T(2,128)}, u32[]{:S(2)}, u32[]{:S(2)}) collective-permute-start(f32[2,30,1024]{2,0,1:T(2,128)} %copy.55), channel_id=1, source_target_pairs={{2,0},{4,2},{6,4},{8,6},{10,8},{12,10},{14,12},{3,1},{5,3},{7,5},{... | collective-permute-start | bytes 737288 | tf_op jit(solution)/shard_map/ppermute | solution.py:24
  7.2 26.0 %collective-permute-start = (f32[2,30,1024]{2,0,1:T(2,128)}, f32[2,30,1024]{2,0,1:T(2,128)S(1)}, u32[]{:S(2)}, u32[]{:S(2)}) collective-permute-start(f32[2,30,1024]{2,0,1:T(2,128)} %copy.54), channel_id=1, source_target_pairs={{0,2},{2,4},{4,6},{6,8},{8,10},{10,12},{12,14},{1,3},{3,5},{5,7},{... | collective-permute-start | bytes 737288 | tf_op jit(solution)/shard_map/ppermute | solution.py:21
  13.6 11.6 %collective-permute-start.10 = (s32[2]{0:T(128)S(1)}, s32[2]{0:T(128)S(1)}, u32[]{:S(2)}, u32[]{:S(2)}) collective-permute-start(s32[2]{0:T(128)S(1)} %get-tuple-element.67), channel_id=1, source_target_pairs={{0,4},{2,6},{4,8},{6,10},{8,12},{10,14},{1,5},{3,7},{5,9},{7,11},{... | collective-permute-start | bytes 32 | tf_op jit(solution)/shard_map/ppermute | solution.py:32
  17.6 9.0 %collective-permute-start.8 = (s32[2]{0:T(128)S(1)}, s32[2]{0:T(128)S(1)}, u32[]{:S(2)}, u32[]{:S(2)}) collective-permute-start(s32[2]{0:T(128)S(1)} %get-tuple-element.66), channel_id=1, source_target_pairs={{0,2},{2,4},{4,6},{6,8},{8,10},{10,12},{12,14},{1,3},{3,5},{5,7},{... | collective-permute-start | bytes 32 | tf_op jit(solution)/shard_map/ppermute | solution.py:32
  21.9 5.5 %collective-permute-start.6 = (s32[2]{0:T(128)S(1)}, s32[2]{0:T(128)S(1)}, u32[]{:S(2)}, u32[]{:S(2)}) collective-permute-start(s32[2]{0:T(128)S(1)} %get-tuple-element.65), channel_id=1, source_target_pairs={{2,0},{4,2},{6,4},{8,6},{10,8},{12,10},{14,12},{3,1},{5,3},{7,5},{... | collective-permute-start | bytes 32 | tf_op jit(solution)/shard_map/ppermute | solution.py:32
  25.2 6.2 %collective-permute-start.4 = (s32[2]{0:T(128)S(1)}, s32[2]{0:T(128)S(1)}, u32[]{:S(2)}, u32[]{:S(2)}) collective-permute-start(s32[2]{0:T(128)S(1)} %get-tuple-element.64), channel_id=1, source_target_pairs={{4,0},{6,2},{8,4},{10,6},{12,8},{14,10},{5,1},{7,3},{9,5},{11,7},{... | collective-permute-start | bytes 32 | tf_op jit(solution)/shard_map/ppermute | solution.py:32
  36.4 9.8 %copy-start = (bf16[4,16,4,1024]{3,2,1,0:T(4,128)(2,1)S(1)}, bf16[4,16,4,1024]{3,2,1,0:T(4,128)(2,1)}, u32[]{:S(2)}) copy-start(bf16[4,16,4,1024]{3,2,1,0:T(4,128)(2,1)} %custom-call.1) | copy-start | bytes 1572868
  36.4 2.9 %collective-permute-start.2 = (f32[2,124,30]{1,2,0:T(8,128)S(1)}, f32[2,124,30]{1,2,0:T(8,128)S(1)}, u32[]{:S(2)}, u32[]{:S(2)}) collective-permute-start(f32[2,124,30]{1,2,0:T(8,128)S(1)} %get-tuple-element.94), channel_id=1, source_target_pairs={{0,1},{2,3},{4,5},{6,7},{8,9},{10,11},{12,13},{14,15},{16,17},{18,... | collective-permute-start | bytes 89288 | tf_op jit(solution)/shard_map/ppermute | solution.py:21
  37.9 3.1 %collective-permute-start.3 = (f32[2,124,30]{1,2,0:T(8,128)S(1)}, f32[2,124,30]{1,2,0:T(8,128)S(1)}, u32[]{:S(2)}, u32[]{:S(2)}) collective-permute-start(f32[2,124,30]{1,2,0:T(8,128)S(1)} %get-tuple-element.93), channel_id=1, source_target_pairs={{1,0},{3,2},{5,4},{7,6},{9,8},{11,10},{13,12},{15,14},{17,16},{19,... | collective-permute-start | bytes 89288 | tf_op jit(solution)/shard_map/ppermute | solution.py:24
  92.5 10.8 %collective-permute-start.11 = (bf16[2,65536]{1,0:T(2,128)(2,1)S(1)}, bf16[2,65536]{1,0:T(2,128)(2,1)S(1)}, u32[]{:S(2)}, u32[]{:S(2)}) collective-permute-start(bf16[2,65536]{1,0:T(2,128)(2,1)S(1)} %convolution_convert_fusion), channel_id=1, source_target_pairs={{0,4},{2,6},{4,8},{6,10},{8,12},{10,14},{1,5},{3,7},{5,9},{7,11},{... | collective-permute-start | bytes 786440 | tf_op jit(solution)/shard_map/ppermute | solution.py:32
  96.7 13.8 %collective-permute-start.9 = (bf16[2,65536]{1,0:T(2,128)(2,1)S(1)}, bf16[2,65536]{1,0:T(2,128)(2,1)S(1)}, u32[]{:S(2)}, u32[]{:S(2)}) collective-permute-start(bf16[2,65536]{1,0:T(2,128)(2,1)S(1)} %convolution_convert_fusion.1), channel_id=1, source_target_pairs={{0,2},{2,4},{4,6},{6,8},{8,10},{10,12},{12,14},{1,3},{3,5},{5,7},{... | collective-permute-start | bytes 786440 | tf_op jit(solution)/shard_map/ppermute | solution.py:32
  99.9 11.0 %collective-permute-start.7 = (bf16[2,65536]{1,0:T(2,128)(2,1)S(1)}, bf16[2,65536]{1,0:T(2,128)(2,1)S(1)}, u32[]{:S(2)}, u32[]{:S(2)}) collective-permute-start(bf16[2,65536]{1,0:T(2,128)(2,1)S(1)} %convolution_convert_fusion.2), channel_id=1, source_target_pairs={{2,0},{4,2},{6,4},{8,6},{10,8},{12,10},{14,12},{3,1},{5,3},{7,5},{... | collective-permute-start | bytes 786440 | tf_op jit(solution)/shard_map/ppermute | solution.py:32
  102.0 14.8 %collective-permute-start.5 = (bf16[2,65536]{1,0:T(2,128)(2,1)S(1)}, bf16[2,65536]{1,0:T(2,128)(2,1)S(1)}, u32[]{:S(2)}, u32[]{:S(2)}) collective-permute-start(bf16[2,65536]{1,0:T(2,128)(2,1)S(1)} %convolution_convert_fusion.3), channel_id=1, source_target_pairs={{4,0},{6,2},{8,4},{10,6},{12,8},{14,10},{5,1},{7,3},{9,5},{11,7},{... | collective-permute-start | bytes 786440 | tf_op jit(solution)/shard_map/ppermute | solution.py:32
where the time goes:
time: 119 us
  starting transfers between devices  30.5 us (26%)
  local copies, waits for them, and re-layouts  28.7 us (24%)
  other arithmetic  28.3 us (24%)
  waiting for transfers between devices  18.5 us (16%)
  matrix products  11.3 us (9%)
    ppermute x8, starting transfers between devices, from_behind(): lax.ppermute(value, axis, [(source, source + steps) for source in range(i...  20.8 us
    ppermute x8, waiting for transfers between devices, from_behind(): lax.ppermute(value, axis, [(source, source + steps) for source in range(i...  16.9 us
    while x4, local copies, waits for them, and re-layouts  11 us
    reduce_sum x4, other arithmetic, correct_block(): coefficient = jnp.sum(node_values * weight_e[None, None], axis=2)  9.71 us
    ppermute x2, starting transfers between devices, with_halo(): lax.ppermute(lax.slice_in_dim(block, block.shape[dim] - width, None, axis...  6.95 us
    while x4, other arithmetic  4.29 us
    dot_general x4, matrix products, correct_block(): jnp.dot(lut_table, joint_weight, preferred_element_type=jnp.float32)  3.91 us
    dynamic_slice x4, local copies, waits for them, and re-layouts, body(): lax.map(correct_block, inputs).reshape(row_count, band_count, col_count)  3.83 us
  transfers between devices with their start and end apart: 12, of which 5 were waited for; matrix products, arithmetic and copies ran while one was open for 7% of the time, Pallas kernels for 0%

commit v1 on v0

v1 whole, which is shorter than its diff:
```python
import functools
import math

import jax
import jax.numpy as jnp
from jax import lax
from jax.experimental import pallas as pl
from jax.experimental.pallas import tpu as pltpu
from jax.sharding import PartitionSpec as P

SEG = 16
REACH = 2
CAP = 2
LANES = 128
MESH_ID = pl.DeviceIdType.MESH
SIDES = [side - REACH for side in range(REACH)] + [side + 1 for side in range(REACH)]
DIRECTIONS = [(da, dc) for da in (-1, 0, 1) for dc in (-1, 0, 1) if (da, dc) != (0, 0)]
f32 = jnp.float32
bf16 = jnp.bfloat16


def split(value):
    high = value.astype(bf16)
    return high, (value - high.astype(f32)).astype(bf16)


def toeplitz(taps, row_count, width, first):
    line = jnp.broadcast_to(taps, (8, taps.shape[1]))
    if width > taps.shape[1]:
        line = jnp.concatenate([line, jnp.zeros((8, width - taps.shape[1]), f32)], axis=1)
    stair = pltpu.roll(line, 0, 1, stride=1, stride_axis=0)
    return jnp.concatenate(
        [pltpu.roll(stair, first + 8 * group, 1) for group in range(row_count // 8)], axis=0
    )


def dot_nt(left, right):
    return lax.dot_general(left, right, (((1,), (1,)), ((), ())), preferred_element_type=f32)


def exists(position, count):
    return (position >= 0) & (position < count)


def both(position_a, count_a, position_c, count_c):
    return exists(position_a, count_a) & exists(position_c, count_c)


def smooth_kernel(
    n_along, n_across, half, levels_a, fields_ref, taps_ref, pos_ref, padded, send_sem, recv_sem
):
    along, across = lax.axis_index("along"), lax.axis_index("across")
    rows, cols = fields_ref.shape[1], fields_ref.shape[2]
    halo = (padded.shape[1] - rows) // 2
    spans = {
        -1: (slice(0, halo), slice(halo + rows, 2 * halo + rows)),
        0: (slice(0, rows), slice(halo, halo + rows)),
        1: (slice(rows - halo, rows), slice(0, halo)),
    }
    lanes = {
        -1: (slice(0, LANES), slice(LANES + cols, 2 * LANES + cols)),
        0: (slice(0, cols), slice(LANES, LANES + cols)),
        1: (slice(cols - LANES, cols), slice(0, LANES)),
    }
    barrier = pltpu.get_barrier_semaphore()
    for da, dc in DIRECTIONS:

        @pl.when(both(along + da, n_along, across + dc, n_across))
        def _():
            pl.semaphore_signal(
                barrier,
                inc=1,
                device_id={"along": along + da, "across": across + dc},
                device_id_type=MESH_ID,
            )

    def describe(number, da, dc):
        return pltpu.make_async_remote_copy(
            src_ref=fields_ref.at[:, spans[da][0], lanes[dc][0]],
            dst_ref=padded.at[:, spans[da][1], lanes[dc][1]],
            send_sem=send_sem.at[number],
            recv_sem=recv_sem.at[number],
            device_id={"along": along + da, "across": across + dc},
            device_id_type=MESH_ID,
        )

    pl.semaphore_wait(
        barrier,
        sum(
            both(along + da, n_along, across + dc, n_across).astype(jnp.int32)
            for da, dc in DIRECTIONS
        ),
    )

    for number, (da, dc) in enumerate(DIRECTIONS):

        @pl.when(both(along + da, n_along, across + dc, n_across))
        def _():
            describe(number, da, dc).start()

    padded[:, spans[0][1], lanes[0][1]] = fields_ref[...]
    for da, dc in DIRECTIONS:

        @pl.when(jnp.logical_not(both(along - da, n_along, across - dc, n_across)))
        def _():
            target = padded.at[:, spans[da][1], lanes[dc][1]]
            target[...] = jnp.zeros(target.shape, bf16)

    down_high, down_low = split(toeplitz(taps_ref[...], rows, 2 * halo + rows, halo - half))
    block = math.gcd(cols, 256)
    across_high, across_low = split(
        toeplitz(taps_ref[...], block, block + 2 * LANES, LANES - half)
    )
    for number, (da, dc) in enumerate(DIRECTIONS):

        @pl.when(both(along - da, n_along, across - dc, n_across))
        def _():
            describe(number, da, dc).wait_recv()

    down = jnp.concatenate([down_high, down_low], axis=0)
    tall = []
    for field in range(2):
        product = jnp.dot(down, padded[field], preferred_element_type=f32)
        tall.append(product[:rows] + product[rows:])
    tall_high, tall_low = split(jnp.concatenate(tall, axis=0))
    for number in range(cols // block):
        window = slice(number * block, number * block + block + 2 * LANES)
        smoothed = dot_nt(tall_high[:, window], across_high)
        smoothed += dot_nt(tall_low[:, window], across_high)
        smoothed += dot_nt(tall_high[:, window], across_low)
        aerosol = smoothed[:rows] / jnp.maximum(smoothed[rows:], 1.0)
        pos_ref[:, number * block : (number + 1) * block] = (levels_a - 1) * jax.nn.sigmoid(
            aerosol
        )
    for number, (da, dc) in enumerate(DIRECTIONS):

        @pl.when(both(along + da, n_along, across + dc, n_across))
        def _():
            describe(number, da, dc).wait_send()


def correct_kernel(
    levels,
    bands,
    routes_ref,
    starts_ref,
    toa_ref,
    pos_ref,
    vapour_ref,
    class_ref,
    frac_ref,
    lut_ref,
    corrected_ref,
    slots_ref,
    tags_ref,
    weights,
    heights,
):
    levels_e, levels_a, levels_w = levels
    seg = pl.program_id(0)
    seg_dev = routes_ref.shape[0]
    own = lax.axis_index("along")
    cols = pos_ref.shape[1]
    seg_rows = SEG * bands

    @pl.when(seg == 0)
    def _():
        slots_ref[...] = jnp.zeros(slots_ref.shape, bf16)
        lane = lax.broadcasted_iota(jnp.int32, (8, CAP * seg_rows), 1)
        for number, side in enumerate(SIDES):
            target = jnp.full((8, CAP * seg_rows), -1, jnp.int32)
            rank = jnp.int32(0)
            for s in range(seg_dev):
                hit = routes_ref[s, 1] - own == side
                place = jnp.where(hit, rank, -1)
                inside = (lane >= place * seg_rows) & (lane < (place + 1) * seg_rows) & (place >= 0)
                target = jnp.where(
                    inside, starts_ref[s, 1] * bands + lane - place * seg_rows, target
                )
                rank = rank + jnp.where(hit, 1, 0)
            tags_ref[number] = target.astype(f32)

    distance = routes_ref[seg, 1] - own
    rank = jnp.int32(0)
    for s in range(seg_dev):
        same = (routes_ref[s, 1] - own == distance) & (s < seg)
        rank = rank + jnp.where(same, 1, 0)
    side_number = jnp.where(distance < 0, distance + REACH, distance + REACH - 1)
    slot = side_number * CAP + rank

    for w in range(levels_w):
        weights[w] = jnp.maximum(0.0, 1.0 - jnp.abs(vapour_ref[...] - float(w)))
    heights[...] = class_ref[...].astype(f32) + frac_ref[...]
    node_a = lax.broadcasted_iota(jnp.int32, (levels_a, cols), 0).astype(f32)
    sub = lax.broadcasted_iota(jnp.int32, (8, cols), 0)
    lower = sub < bands
    pair_e = (sub // bands).astype(f32)
    per_tile = 8 // bands
    lut = lut_ref[...]
    quad = 16 // bands
    table_rows = levels_e * bands
    for first in range(0, SEG, quad):
        partial = []
        for row in range(first, first + quad):
            weight_a = jnp.maximum(0.0, 1.0 - jnp.abs(pos_ref[row : row + 1, :] - node_a)).astype(
                bf16
            )
            joint = jnp.concatenate(
                [
                    weight_a
                    * jnp.broadcast_to(weights[w, row : row + 1, :], (levels_a, cols)).astype(bf16)
                    for w in range(levels_w)
                ],
                axis=0,
            )
            nodes = jnp.dot(lut, joint, preferred_element_type=f32)
            height = heights[row : row + 1, :]
            sums = [None] * 3
            for k in range(table_rows // 8):
                weight_e = jnp.maximum(0.0, 1.0 - jnp.abs(height - (pair_e + float(per_tile * k))))
                for t in range(3):
                    at = t * table_rows + k * 8
                    term = nodes[at : at + 8] * weight_e
                    sums[t] = term if sums[t] is None else sums[t] + term
            partial.append(sums)
        radiance = toa_ref[first * bands : (first + quad) * bands, :].astype(f32)
        surfaces = []
        for half in range(quad // 2):
            coefficient = []
            for t in range(3):
                one, two = partial[2 * half][t], partial[2 * half + 1][t]
                kept = jnp.where(lower, one, two)
                moved = pltpu.roll(jnp.where(lower, two, one), bands, 0)
                coefficient.append(kept + moved)
            scaled = coefficient[0] * radiance[half * 8 : half * 8 + 8] - coefficient[1]
            surfaces.append(scaled / (1.0 + coefficient[2] * scaled))
        surface = jnp.concatenate(surfaces, axis=0).astype(bf16)
        corrected_ref[seg, first * bands : (first + quad) * bands, :] = surface
        slots_ref[slot, first * bands : (first + quad) * bands, :] = surface


def place_kernel(
    n_along,
    bands,
    routes_ref,
    starts_ref,
    corrected_ref,
    slots_ref,
    tags_ref,
    out_ref,
    got_rows,
    got_tags,
    send_sem,
    recv_sem,
):
    along = lax.axis_index("along")
    barrier = pltpu.get_barrier_semaphore()
    seg_dev, seg_rows = corrected_ref.shape[0], corrected_ref.shape[1]
    cols = corrected_ref.shape[2]
    out_rows = out_ref.shape[0]
    for side in SIDES:

        @pl.when(exists(along + side, n_along))
        def _():
            pl.semaphore_signal(
                barrier, inc=1, device_id={"along": along + side}, device_id_type=MESH_ID
            )

    pl.semaphore_wait(
        barrier, sum(exists(along + side, n_along).astype(jnp.int32) for side in SIDES)
    )

    def describe(number):
        side = SIDES[number]
        rows = pltpu.make_async_remote_copy(
            src_ref=slots_ref.at[pl.ds(number * CAP, CAP)],
            dst_ref=got_rows.at[number],
            send_sem=send_sem.at[number],
            recv_sem=recv_sem.at[number],
            device_id={"along": along + side},
            device_id_type=MESH_ID,
        )
        tags = pltpu.make_async_remote_copy(
            src_ref=tags_ref.at[number],
            dst_ref=got_tags.at[number],
            send_sem=send_sem.at[len(SIDES) + number],
            recv_sem=recv_sem.at[len(SIDES) + number],
            device_id={"along": along + side},
            device_id_type=MESH_ID,
        )
        return tags, rows

    order = sorted(range(len(SIDES)), key=lambda number: abs(SIDES[number]))
    for number in order:

        @pl.when(exists(along + SIDES[number], n_along))
        def _():
            for copy in describe(number):
                copy.start()

        @pl.when(jnp.logical_not(exists(along - SIDES[number], n_along)))
        def _():
            got_rows[number] = jnp.zeros(got_rows.shape[1:], bf16)
            got_tags[number] = jnp.full(got_tags.shape[1:], -1.0, f32)

    def placed(target):
        row = lax.broadcasted_iota(jnp.int32, (out_rows, target.shape[1]), 0).astype(f32)
        return jnp.where(row == target, 1.0, 0.0)

    lane = lax.broadcasted_iota(jnp.int32, (1, seg_dev * seg_rows), 1)
    target = jnp.full((1, seg_dev * seg_rows), -1, jnp.int32)
    for s in range(seg_dev):
        inside = (lane >= s * seg_rows) & (lane < (s + 1) * seg_rows)
        inside = inside & (routes_ref[s, 0] == along)
        target = jnp.where(inside, starts_ref[s, 0] * bands + lane - s * seg_rows, target)
    matrix = placed(target.astype(f32))
    count = jnp.sum(matrix, axis=1, keepdims=True)
    summed = jnp.dot(
        matrix.astype(bf16),
        corrected_ref[...].reshape(seg_dev * seg_rows, cols),
        preferred_element_type=f32,
    )
    for number in order:

        @pl.when(exists(along - SIDES[number], n_along))
        def _():
            for copy in describe(number):
                copy.wait_recv()

        matrix = placed(got_tags[number, 0:1, :])
        count = count + jnp.sum(matrix, axis=1, keepdims=True)
        summed = summed + jnp.dot(
            matrix.astype(bf16),
            got_rows[number].reshape(CAP * seg_rows, cols),
            preferred_element_type=f32,
        )
    out_ref[...] = (summed / jnp.maximum(count, 1.0)).astype(bf16)
    for number in order:

        @pl.when(exists(along + SIDES[number], n_along))
        def _():
            for copy in describe(number):
                copy.wait_send()


def body(
    n_along,
    n_across,
    toa_bands,
    dark_mask,
    vapour,
    elev_class,
    elev_frac,
    kernel,
    lut_gain,
    lut_path,
    lut_albedo,
    routes,
    starts,
):
    rows, bands, cols = toa_bands.shape
    half = kernel.shape[0] // 2
    halo = -(-half // 16) * 16
    levels = lut_gain.shape[1:]
    levels_e, levels_a, levels_w = levels
    seg_dev = routes.shape[0]
    seg_rows = SEG * bands
    side_count = len(SIDES)
    vmem = pl.BlockSpec(memory_space=pltpu.VMEM)
    smem = pl.BlockSpec(memory_space=pltpu.SMEM)

    darkness = dark_mask.astype(f32)
    weighted = darkness * 8.0 * (toa_bands[:, 0, :].astype(f32) - 0.5 * toa_bands[:, 2, :].astype(f32))
    fields = jnp.stack([weighted, darkness]).astype(bf16)
    taps = jnp.pad(kernel, (0, LANES - kernel.shape[0]))[None]
    lut = (
        jnp.stack([lut_gain, lut_path, lut_albedo])
        .transpose(0, 2, 1, 4, 3)
        .reshape(3 * levels_e * bands, levels_w * levels_a)
    )
    flat = toa_bands.reshape(rows * bands, cols)

    aero_pos = pl.pallas_call(
        functools.partial(smooth_kernel, n_along, n_across, half, levels_a),
        out_shape=jax.ShapeDtypeStruct((rows, cols), f32),
        in_specs=[vmem, vmem],
        out_specs=vmem,
        scratch_shapes=[
            pltpu.VMEM((2, rows + 2 * halo, cols + 2 * LANES), bf16),
            pltpu.SemaphoreType.DMA((len(DIRECTIONS),)),
            pltpu.SemaphoreType.DMA((len(DIRECTIONS),)),
        ],
        compiler_params=pltpu.CompilerParams(collective_id=0, has_side_effects=True),
        name="smooth",
    )(fields, taps)

    def rows_spec(count):
        return pl.BlockSpec((count, cols), lambda s: (s, 0))

    corrected, slots, tags = pl.pallas_call(
        functools.partial(correct_kernel, levels, bands),
        grid=(seg_dev,),
        out_shape=(
            jax.ShapeDtypeStruct((seg_dev, seg_rows, cols), bf16),
            jax.ShapeDtypeStruct((side_count * CAP, seg_rows, cols), bf16),
            jax.ShapeDtypeStruct((side_count, 8, CAP * seg_rows), f32),
        ),
        in_specs=[
            smem,
            smem,
            rows_spec(seg_rows),
            rows_spec(SEG),
            rows_spec(SEG),
            rows_spec(SEG),
            rows_spec(SEG),
            vmem,
        ],
        out_specs=(vmem, vmem, vmem),
        scratch_shapes=[
            pltpu.VMEM((levels_w, SEG, cols), f32),
            pltpu.VMEM((SEG, cols), f32),
        ],
        compiler_params=pltpu.CompilerParams(dimension_semantics=("arbitrary",)),
        name="correct",
    )(routes, starts, flat, aero_pos, vapour, elev_class, elev_frac, lut)

    out = pl.pallas_call(
        functools.partial(place_kernel, n_along, bands),
        out_shape=jax.ShapeDtypeStruct((rows * bands, cols), bf16),
        in_specs=[smem, smem, vmem, vmem, vmem],
        out_specs=vmem,
        scratch_shapes=[
            pltpu.VMEM((side_count, CAP, seg_rows, cols), bf16),
            pltpu.VMEM((side_count, 8, CAP * seg_rows), f32),
            pltpu.SemaphoreType.DMA((2 * side_count,)),
            pltpu.SemaphoreType.DMA((2 * side_count,)),
        ],
        compiler_params=pltpu.CompilerParams(collective_id=1, has_side_effects=True),
        name="place",
    )(routes, starts, corrected, slots, tags)
    return out.reshape(1, rows, bands, cols)


def solution(mesh):
    in_specs = (
        P(("groups", "along"), None, "across"),
        P(("groups", "along"), "across"),
        P(("groups", "along"), "across"),
        P(("groups", "along"), "across"),
        P(("groups", "along"), "across"),
        P(),
        P(),
        P(),
        P(),
        P(("groups", "along"), None),
        P(("groups", "along"), None),
    )
    out_specs = P(("groups", "along"), None, None, "across")
    run = functools.partial(body, mesh.shape["along"], mesh.shape["across"])
    return jax.shard_map(run, mesh=mesh, in_specs=in_specs, out_specs=out_specs, check_vma=False)
```

time: 119 us -> 52.7 us (0.44)
  Pallas kernels: 0 us -> 42.8 us
  starting transfers between devices: 30.5 us -> 0 us
  other arithmetic: 28.3 us -> 1.91 us
  local copies, waits for them, and re-layouts: 28.7 us -> 7.56 us
  waiting for transfers between devices: 18.5 us -> 0 us
  matrix products: 11.3 us -> 0 us
    pallas_call x0 -> x3, Pallas kernels: none -> 42.8 us  [the longest x1 21 us: body(): pl.pallas_call(functools.partial(place_kernel, n_along, bands), out_shape...]
    ppermute x12 -> x0, starting transfers between devices: 30.5 us -> none  [the longest x8 20.8 us: from_behind(): lax.ppermute(value, axis, [(source, source + steps) for source in range(i...]
    ppermute x12 -> x0, waiting for transfers between devices: 18.5 us -> none  [the longest x8 16.9 us: from_behind(): lax.ppermute(value, axis, [(source, source + steps) for source in range(i...]
    reduce_sum x12 -> x0, other arithmetic: 11.4 us -> none  [the longest x4 9.71 us: correct_block(): coefficient = jnp.sum(node_values * weight_e[None, None], axis=2)]
    dot_general x22 -> x0, matrix products: 11.3 us -> none  [the longest x4 3.91 us: correct_block(): jnp.dot(lut_table, joint_weight, preferred_element_type=jnp.float32)]
    while x4 -> x0, local copies, waits for them, and re-layouts: 11 us -> none
    while x4 -> x0, other arithmetic: 4.29 us -> none
    broadcast_in_dim x9 -> x0, other arithmetic: 4.01 us -> none  [the longest x4 3.56 us: correct_block(): jnp.where(elev_ids == class_block[None], 1.0 - frac_block[None], 0.0)]
  transfers between devices with their start and end apart: 12 -> 0, of which waited for: 5 -> 0; matrix products, arithmetic and copies ran while one was open for 7% -> 0% of each run, Pallas kernels for 0% -> 0%
where the time goes in v1:
time: 52.7 us; the launch traced here: 52.4 us
  Pallas kernels  42.8 us (81%)
  local copies, waits for them, and re-layouts  7.56 us (14%)
  other arithmetic  1.91 us (4%)
    pallas_call x1, Pallas kernels, body(): pl.pallas_call(functools.partial(place_kernel, n_along, bands), out_shape...  21 us
    pallas_call x1, Pallas kernels, body(): pl.pallas_call(functools.partial(smooth_kernel, n_along, n_across, half,...  11.6 us
    pallas_call x1, Pallas kernels, body(): pl.pallas_call(functools.partial(correct_kernel, levels, bands), grid=(se...  10.2 us
    unnamed x18, local copies, waits for them, and re-layouts  2.87 us
    reshape x1, local copies, waits for them, and re-layouts, body(): return out.reshape(1, rows, bands, cols)  2.03 us
    another operation x3, other arithmetic, body(): fields = jnp.stack([weighted, darkness]).astype(bf16)  1.86 us

profile of v1, /device:TPU:0, one launch (start us, length us, event | category | flops | bytes accessed | tf_op | source)
XLA Modules:
  0.0 52.4 jit_solution(7267596529109498195)
XLA Ops:
  0.0 0.0 copy-start.7
  0.0 0.7 %copy-done.7 = f32[61]{0:T(128)S(1)} copy-done((f32[61]{0:T(128)S(1)}, f32[61]{0:T(128)}, u32[]{:S(2)}) %copy-start.7) | copy-done | bytes 268
  0.7 0.0 copy-start.5
  0.7 0.6 %pad_bitcast_fusion.taps_ref = f32[1,128]{1,0:T(1,128)} fusion(f32[61]{0:T(128)S(1)} %copy-done.7), kind=kLoop, calls=%fused_computation.7 | loop fusion | bytes 756 | tf_op jit(solution)/shard_map/broadcast_in_dim | solution.py:375
  1.2 0.1 copy-done.5
  1.3 0.0 copy-start.6
  1.3 0.7 %copy.17.routes_ref = s32[4,2]{1,0:T(4,128)} copy(s32[4,2]{0,1:T(2,128)S(1)} %copy-done.5) | data formatting | bytes 64 | tf_op args[9]
  2.0 0.0 copy-done.6
  2.0 0.7 %copy.18.starts_ref = s32[4,2]{1,0:T(4,128)} copy(s32[4,2]{0,1:T(2,128)S(1)} %copy-done.6) | data formatting | bytes 64 | tf_op args[10]
  2.7 0.0 copy-start.2
  2.7 0.0 copy-start.3
  2.7 0.0 copy-start.4
  2.7 1.0 %fusion.1 = bf16[1,64,1024]{2,1,0:T(8,128)(2,1)S(1)} fusion(s32[64,1024]{1,0:T(8,128)} %param.12), kind=kLoop, calls=%fused_computation.5 | loop fusion | flops 131072 | bytes 393216 | tf_op jit(solution)/shard_map/stack | solution.py:374
  3.7 0.0 copy-done.2
  3.7 0.0 copy-done.3
  3.7 0.0 copy-done.4
  3.7 0.0 copy-start
  3.8 0.8 %reshape.15.lut_ref = bf16[96,128]{1,0:T(8,128)(2,1)} reshape(bf16[3,8,4,8,16]{4,3,2,1,0:T(8,128)(2,1)S(1)} %copy.14) | data formatting | bytes 49152 | tf_op jit(solution)/shard_map/reshape | solution.py:379
  4.6 0.2 copy-done
  4.8 0.9 %reshape.14.toa_ref = bf16[256,1024]{1,0:T(8,128)(2,1)} reshape(bf16[64,4,1024]{2,1,0:T(4,128)(2,1)S(1)} %copy-done) | data formatting | bytes 1048576 | tf_op jit(solution)/shard_map/reshape | solution.py:381
  5.7 0.0 copy-start.1
  5.7 0.4 fusion.3
  6.1 0.6 %copy-done.1 = s32[64,1024]{1,0:T(8,128)S(1)} copy-done((s32[64,1024]{1,0:T(8,128)S(1)}, s32[64,1024]{1,0:T(8,128)}, u32[]{:S(2)}) %copy-start.1) | copy-done | bytes 262168
  6.6 0.1 fusion.2
  6.8 0.7 %pad_maximum_fusion.fields_ref = bf16[2,64,1024]{2,1,0:T(8,128)(2,1)} fusion(bf16[1,64,1024]{2,1,0:T(8,128)(2,1)S(1)} %fusion.1, bf16[1,64,1024]{2,1,0:T(8,128)(2,1)S(1)} %fusion.2), kind=kLoop, calls=%fused_computation | loop fusion | flops 131072 | bytes 524288 | tf_op jit(solution)/shard_map/stack | solution.py:374
  7.5 11.6 %smooth.1.pos_ref = f32[64,1024]{1,0:T(8,128)} custom-call(bf16[2,64,1024]{2,1,0:T(8,128)(2,1)} %pad_maximum_fusion.fields_ref, f32[1,128]{1,0:T(1,128)} %pad_bitcast_fusion.taps_ref), custom_call_target="tpu_custom_call" | custom-call | tf_op jit(solution)/shard_map/smooth/pallas_call | solution.py:383
  19.1 10.2 %correct.1 = (bf16[4,64,1024]{2,1,0:T(8,128)(2,1)}, bf16[8,64,1024]{2,1,0:T(8,128)(2,1)}, f32[4,8,128]{2,1,0:T(8,128)}) custom-call(s32[4,2]{1,0:T(4,128)} %copy.17.routes_ref, s32[4,2]{1,0:T(4,128)} %copy.18.starts_ref, bf16[256,1024]{1,0:T(8,128)(2,1)} %reshape.14.toa_ref, f32[64,1024]{1,0:T(8,128)} %smooth.1.pos_ref, f32[64,1024]{1,0:T(8,128)} %vapour_ref.1, ...), custom_call_target="tpu_custom_call" | custom-call | tf_op jit(solution)/shard_map/correct/pallas_call | solution.py:400
  29.3 21.0 %place.1 = bf16[256,1024]{1,0:T(8,128)(2,1)} custom-call(s32[4,2]{1,0:T(4,128)} %copy.17.routes_ref, s32[4,2]{1,0:T(4,128)} %copy.18.starts_ref, bf16[4,64,1024]{2,1,0:T(8,128)(2,1)} %get-tuple-element.8.corrected_ref, bf16[8,64,1024]{2,1,0:T(8,128)(2,1)} %get-tuple-element.9.slots_ref, f32[4,8,128]{2,1,0:T(8,128)} %get-tuple-element.10.tags_ref), custom_call_target="tpu_custom_call" | custom-call | tf_op jit(solution)/shard_map/place/pallas_call | solution.py:427
  50.3 2.0 %reshape.16 = bf16[1,64,4,1024]{3,2,1,0:T(4,128)(2,1)} reshape(bf16[256,1024]{1,0:T(8,128)(2,1)} %place.1) | data formatting | bytes 1048576 | tf_op jit(solution)/shard_map/reshape | solution.py:441
  (2 shorter events, 0.1 us)
Async XLA Ops:
  0.0 0.7 %copy-start.7 = (f32[61]{0:T(128)S(1)}, f32[61]{0:T(128)}, u32[]{:S(2)}) copy-start(f32[61]{0:T(128)} %param.16) | copy-start | bytes 736
  0.7 0.7 %copy-start.5 = (s32[4,2]{0,1:T(2,128)S(1)}, s32[4,2]{0,1:T(2,128)}, u32[]{:S(2)}) copy-start(s32[4,2]{0,1:T(2,128)} %param.20) | copy-start | bytes 100
  1.3 0.7 %copy-start.6 = (s32[4,2]{0,1:T(2,128)S(1)}, s32[4,2]{0,1:T(2,128)}, u32[]{:S(2)}) copy-start(s32[4,2]{0,1:T(2,128)} %param.21) | copy-start | bytes 100
  2.7 1.0 %copy-start.2 = (bf16[4,8,16,8]{2,3,1,0:T(8,128)(2,1)S(1)}, bf16[4,8,16,8]{2,3,1,0:T(8,128)(2,1)}, u32[]{:S(2)}) copy-start(bf16[4,8,16,8]{2,3,1,0:T(8,128)(2,1)} %param.19) | copy-start | bytes 24580
  2.7 1.0 %copy-start.3 = (bf16[4,8,16,8]{2,3,1,0:T(8,128)(2,1)S(1)}, bf16[4,8,16,8]{2,3,1,0:T(8,128)(2,1)}, u32[]{:S(2)}) copy-start(bf16[4,8,16,8]{2,3,1,0:T(8,128)(2,1)} %param.18) | copy-start | bytes 24580
  2.7 1.0 %copy-start.4 = (bf16[4,8,16,8]{2,3,1,0:T(8,128)(2,1)S(1)}, bf16[4,8,16,8]{2,3,1,0:T(8,128)(2,1)}, u32[]{:S(2)}) copy-start(bf16[4,8,16,8]{2,3,1,0:T(8,128)(2,1)} %param.17) | copy-start | bytes 24580
  3.7 1.0 %copy-start = (bf16[64,4,1024]{2,1,0:T(4,128)(2,1)S(1)}, bf16[64,4,1024]{2,1,0:T(4,128)(2,1)}, u32[]{:S(2)}) copy-start(bf16[64,4,1024]{2,1,0:T(4,128)(2,1)} %param.11) | copy-start | bytes 1572868
  5.7 0.9 %copy-start.1 = (s32[64,1024]{1,0:T(8,128)S(1)}, s32[64,1024]{1,0:T(8,128)}, u32[]{:S(2)}) copy-start(s32[64,1024]{1,0:T(8,128)} %param.12) | copy-start | bytes 786436

commit v2 on v0

v2 whole, which is shorter than its diff:
```python
import functools
import math

import jax
import jax.numpy as jnp
from jax import lax
from jax.experimental import pallas as pl
from jax.experimental.pallas import tpu as pltpu
from jax.sharding import PartitionSpec as P

SEG = 16
REACH = 2
CAP = 2
LANES = 128
MESH_ID = pl.DeviceIdType.MESH
SIDES = [side - REACH for side in range(REACH)] + [side + 1 for side in range(REACH)]
DIRECTIONS = [(da, dc) for da in (-1, 0, 1) for dc in (-1, 0, 1) if (da, dc) != (0, 0)]
f32 = jnp.float32
bf16 = jnp.bfloat16


def split(value):
    high = value.astype(bf16)
    return high, (value - high.astype(f32)).astype(bf16)


def toeplitz(taps, row_count, width, first):
    line = jnp.broadcast_to(taps, (8, taps.shape[1]))
    if width > taps.shape[1]:
        line = jnp.concatenate([line, jnp.zeros((8, width - taps.shape[1]), f32)], axis=1)
    stair = pltpu.roll(line, 0, 1, stride=1, stride_axis=0)
    return jnp.concatenate(
        [pltpu.roll(stair, first + 8 * group, 1) for group in range(row_count // 8)], axis=0
    )


def dot_nt(left, right):
    return lax.dot_general(left, right, (((1,), (1,)), ((), ())), preferred_element_type=f32)


def exists(position, count):
    return (position >= 0) & (position < count)


def both(position_a, count_a, position_c, count_c):
    return exists(position_a, count_a) & exists(position_c, count_c)


def prep_kernel(toa_ref, mask_ref, routes_ref, starts_ref, flat_ref, fields_ref, tags_ref):
    rows, bands, cols = toa_ref.shape
    own = lax.axis_index("along")
    flat = toa_ref[...].astype(f32).reshape(rows * bands, cols).astype(bf16)
    flat_ref[...] = flat
    row = lax.broadcasted_iota(jnp.int32, (rows, rows * bands), 0) * bands
    col = lax.broadcasted_iota(jnp.int32, (rows, rows * bands), 1)
    pick = jnp.where(col == row, 8.0, 0.0) + jnp.where(col == row + 2, -4.0, 0.0)
    darkness = mask_ref[...].astype(f32)
    value = jnp.dot(pick.astype(bf16), flat, preferred_element_type=f32)
    fields_ref[0] = (darkness * value).astype(bf16)
    fields_ref[1] = darkness.astype(bf16)
    seg_rows = SEG * bands
    lane = lax.broadcasted_iota(jnp.int32, (8, CAP * seg_rows), 1)
    for number, side in enumerate(SIDES):
        target = jnp.full((8, CAP * seg_rows), -1, jnp.int32)
        rank = jnp.int32(0)
        for s in range(routes_ref.shape[1]):
            hit = routes_ref[1, s] - own == side
            place = jnp.where(hit, rank, -1)
            inside = (lane >= place * seg_rows) & (lane < (place + 1) * seg_rows) & (place >= 0)
            target = jnp.where(inside, starts_ref[1, s] * bands + lane - place * seg_rows, target)
            rank = rank + jnp.where(hit, 1, 0)
        tags_ref[number] = target.astype(f32)


def main_kernel(
    n_along,
    n_across,
    bands,
    levels,
    routes_ref,
    starts_ref,
    fields_ref,
    tags_ref,
    taps_ref,
    gain_ref,
    path_ref,
    albedo_ref,
    toa_hbm,
    vapour_hbm,
    class_hbm,
    frac_hbm,
    out_ref,
    toa_ref,
    vapour_ref,
    class_ref,
    frac_ref,
    taps_pad,
    padded,
    pos_ref,
    weights,
    heights,
    corrected,
    slots,
    got_rows,
    got_tags,
    load_sem,
    halo_send,
    halo_recv,
    tag_send,
    tag_recv,
    slot_send,
    slot_recv,
):
    along, across = lax.axis_index("along"), lax.axis_index("across")
    levels_e, levels_a, levels_w = levels
    rows, cols = fields_ref.shape[1], fields_ref.shape[2]
    halo = (padded.shape[1] - rows) // 2
    half = taps_ref.shape[1] // 2
    chunks, seg_dev, seg_rows, width = corrected.shape
    loads = [
        pltpu.make_async_copy(source, target, load_sem.at[number])
        for number, (source, target) in enumerate(
            (
                (vapour_hbm, vapour_ref),
                (class_hbm, class_ref),
                (frac_hbm, frac_ref),
                (toa_hbm, toa_ref),
            )
        )
    ]
    barrier = pltpu.get_barrier_semaphore()
    peers = DIRECTIONS + [(side, 0) for side in SIDES if (side, 0) not in DIRECTIONS]
    for da, dc in peers:

        @pl.when(both(along + da, n_along, across + dc, n_across))
        def _():
            pl.semaphore_signal(
                barrier,
                inc=1,
                device_id={"along": along + da, "across": across + dc},
                device_id_type=MESH_ID,
            )

    for load in loads:
        load.start()
    spans = {
        -1: (slice(0, halo), slice(halo + rows, 2 * halo + rows)),
        0: (slice(0, rows), slice(halo, halo + rows)),
        1: (slice(rows - halo, rows), slice(0, halo)),
    }
    lanes = {
        -1: (slice(0, LANES), slice(LANES + cols, 2 * LANES + cols)),
        0: (slice(0, cols), slice(LANES, LANES + cols)),
        1: (slice(cols - LANES, cols), slice(0, LANES)),
    }

    def halo_copy(number, da, dc):
        return pltpu.make_async_remote_copy(
            src_ref=fields_ref.at[:, spans[da][0], lanes[dc][0]],
            dst_ref=padded.at[:, spans[da][1], lanes[dc][1]],
            send_sem=halo_send.at[number],
            recv_sem=halo_recv.at[number],
            device_id={"along": along + da, "across": across + dc},
            device_id_type=MESH_ID,
        )

    def tag_copy(number):
        return pltpu.make_async_remote_copy(
            src_ref=tags_ref.at[number],
            dst_ref=got_tags.at[number],
            send_sem=tag_send.at[number],
            recv_sem=tag_recv.at[number],
            device_id={"along": along + SIDES[number]},
            device_id_type=MESH_ID,
        )

    def slot_copy(chunk, number):
        return pltpu.make_async_remote_copy(
            src_ref=slots.at[chunk, pl.ds(number * CAP, CAP)],
            dst_ref=got_rows.at[chunk, number],
            send_sem=slot_send.at[chunk, number],
            recv_sem=slot_recv.at[chunk, number],
            device_id={"along": along + SIDES[number]},
            device_id_type=MESH_ID,
        )

    pl.semaphore_wait(
        barrier,
        sum(
            both(along + da, n_along, across + dc, n_across).astype(jnp.int32) for da, dc in peers
        ),
    )
    for number, (da, dc) in enumerate(DIRECTIONS):

        @pl.when(both(along + da, n_along, across + dc, n_across))
        def _():
            halo_copy(number, da, dc).start()

    order = sorted(range(len(SIDES)), key=lambda number: abs(SIDES[number]))
    for number in order:

        @pl.when(exists(along + SIDES[number], n_along))
        def _():
            tag_copy(number).start()

        @pl.when(jnp.logical_not(exists(along - SIDES[number], n_along)))
        def _():
            got_rows[:, number] = jnp.zeros((chunks, CAP, seg_rows, width), bf16)
            got_tags[number] = jnp.full(got_tags.shape[1:], -1.0, f32)

    padded[:, spans[0][1], lanes[0][1]] = fields_ref[...]
    for da, dc in DIRECTIONS:

        @pl.when(jnp.logical_not(both(along - da, n_along, across - dc, n_across)))
        def _():
            target = padded.at[:, spans[da][1], lanes[dc][1]]
            target[...] = jnp.zeros(target.shape, bf16)

    taps_pad[...] = jnp.zeros(taps_pad.shape, f32)
    taps_pad[0:1, 0 : taps_ref.shape[1]] = taps_ref[...]
    taps = taps_pad[0:1, :]
    down_high, down_low = split(toeplitz(taps, rows, 2 * halo + rows, halo - half))
    down = jnp.concatenate([down_high, down_low], axis=0)
    block = width
    across_high, across_low = split(toeplitz(taps, block, block + 2 * LANES, LANES - half))

    node_count = levels_w * levels_a
    tables = jnp.concatenate([gain_ref[...], path_ref[...], albedo_ref[...]], axis=0)
    spread_a = lax.broadcasted_iota(jnp.int32, (levels_a, node_count), 0)
    spread_n = lax.broadcasted_iota(jnp.int32, (levels_a, node_count), 1)
    spread = jnp.where(spread_n % levels_a == spread_a, 1.0, 0.0).astype(bf16)
    wide = jnp.dot(tables, spread, preferred_element_type=f32)
    wide_w = lax.broadcasted_iota(jnp.int32, wide.shape, 0) % levels_w
    wide_n = lax.broadcasted_iota(jnp.int32, wide.shape, 1) // levels_a
    wide = jnp.where(wide_w == wide_n, wide, 0.0).astype(bf16)
    table_rows = levels_e * bands
    into = lax.broadcasted_iota(jnp.int32, (3 * table_rows, wide.shape[0]), 0)
    source = lax.broadcasted_iota(jnp.int32, (3 * table_rows, wide.shape[0]), 1) // levels_w
    within = into % table_rows
    wanted = into - within + (within % bands) * levels_e + within // bands
    lut = jnp.dot(
        jnp.where(source == wanted, 1.0, 0.0).astype(bf16), wide, preferred_element_type=f32
    ).astype(bf16)

    for load in loads:
        load.wait()
    for w in range(levels_w):
        weights[w] = jnp.maximum(0.0, 1.0 - jnp.abs(vapour_ref[...] - float(w)))
    heights[...] = class_ref[...].astype(f32) + frac_ref[...]

    for number, (da, dc) in enumerate(DIRECTIONS):

        @pl.when(both(along - da, n_along, across - dc, n_across))
        def _():
            halo_copy(number, da, dc).wait_recv()

    tall = []
    for field in range(2):
        product = jnp.dot(down, padded[field], preferred_element_type=f32)
        tall.append(product[:rows] + product[rows:])
    tall_high, tall_low = split(jnp.concatenate(tall, axis=0))
    for number in range(chunks):
        window = slice(number * block, number * block + block + 2 * LANES)
        smoothed = dot_nt(tall_high[:, window], across_high)
        smoothed += dot_nt(tall_low[:, window], across_high)
        smoothed += dot_nt(tall_high[:, window], across_low)
        aerosol = smoothed[:rows] / jnp.maximum(smoothed[rows:], 1.0)
        pos_ref[:, number * block : (number + 1) * block] = (levels_a - 1) * jax.nn.sigmoid(
            aerosol
        )

    chosen = []
    for number, side in enumerate(SIDES):
        rank = jnp.int32(0)
        first = [jnp.int32(0) for _ in range(CAP)]
        for s in range(seg_dev):
            hit = routes_ref[1, s] - along == side
            for k in range(CAP):
                first[k] = jnp.where(hit & (rank == k), s, first[k])
            rank = rank + jnp.where(hit, 1, 0)
        chosen.append(first)

    node_a = lax.broadcasted_iota(jnp.int32, (levels_a, width), 0).astype(f32)
    sub = lax.broadcasted_iota(jnp.int32, (8, width), 0)
    lower = sub < bands
    pair_e = (sub // bands).astype(f32)
    per_tile = 8 // bands
    quad = 16 // bands

    def correct(chunk, seg):
        at_cols = slice(chunk * width, (chunk + 1) * width)
        base = pl.multiple_of(seg * SEG, SEG)
        base_flat = pl.multiple_of(seg * seg_rows, seg_rows)
        position = pos_ref[pl.ds(base, SEG), at_cols]
        height_rows = heights[pl.ds(base, SEG), at_cols]
        for first in range(0, SEG, quad):
            partial = []
            for row in range(first, first + quad):
                weight_a = jnp.maximum(0.0, 1.0 - jnp.abs(position[row : row + 1] - node_a))
                joint = jnp.concatenate(
                    [
                        (weight_a * weights[w, pl.ds(base + row, 1), at_cols]).astype(bf16)
                        for w in range(levels_w)
                    ],
                    axis=0,
                )
                nodes = jnp.dot(lut, joint, preferred_element_type=f32)
                height = height_rows[row : row + 1]
                sums = [None] * 3
                for k in range(table_rows // 8):
                    weight_e = jnp.maximum(
                        0.0, 1.0 - jnp.abs(height - (pair_e + float(per_tile * k)))
                    )
                    for t in range(3):
                        at = t * table_rows + k * 8
                        term = nodes[at : at + 8] * weight_e
                        sums[t] = term if sums[t] is None else sums[t] + term
                partial.append(sums)
            radiance = toa_ref[pl.ds(base_flat + first * bands, quad * bands), at_cols].astype(f32)
            surfaces = []
            for part in range(quad // 2):
                coefficient = []
                for t in range(3):
                    one, two = partial[2 * part][t], partial[2 * part + 1][t]
                    kept = jnp.where(lower, one, two)
                    moved = pltpu.roll(jnp.where(lower, two, one), bands, 0)
                    coefficient.append(kept + moved)
                scaled = coefficient[0] * radiance[part * 8 : part * 8 + 8] - coefficient[1]
                surfaces.append(scaled / (1.0 + coefficient[2] * scaled))
            corrected[chunk, seg, first * bands : (first + quad) * bands, :] = jnp.concatenate(
                surfaces, axis=0
            ).astype(bf16)

    def correct_from(chunk, low, high):
        def step(seg, carry):
            correct(chunk, seg)
            return carry

        lax.fori_loop(low, high, step, 0)

    def start_slots(chunk):
        for number in order:

            @pl.when(exists(along + SIDES[number], n_along))
            def _():
                slot_copy(chunk, number).start()

    def placed(target):
        row = lax.broadcasted_iota(jnp.int32, (rows * bands, target.shape[1]), 0).astype(f32)
        return jnp.where(row == target, 1.0, 0.0)

    for chunk in range(chunks):
        correct_from(chunk, 0, 1)
        if chunk:
            start_slots(chunk - 1)
        correct_from(chunk, 1, seg_dev)
        for number in range(len(SIDES)):
            for k in range(CAP):
                slots[chunk, number * CAP + k] = corrected[chunk, chosen[number][k]]

    lane = lax.broadcasted_iota(jnp.int32, (1, seg_dev * seg_rows), 1)
    target = jnp.full((1, seg_dev * seg_rows), -1, jnp.int32)
    for s in range(seg_dev):
        inside = (lane >= s * seg_rows) & (lane < (s + 1) * seg_rows)
        inside = inside & (routes_ref[0, s] == along)
        target = jnp.where(inside, starts_ref[0, s] * bands + lane - s * seg_rows, target)
    own = placed(target.astype(f32))
    start_slots(chunks - 1)
    count = jnp.sum(own, axis=1, keepdims=True)
    own = own.astype(bf16)
    matrices = {}
    for number in order:

        @pl.when(exists(along - SIDES[number], n_along))
        def _():
            tag_copy(number).wait_recv()

        matrix = placed(got_tags[number, 0:1, :])
        count = count + jnp.sum(matrix, axis=1, keepdims=True)
        matrices[number] = matrix.astype(bf16)
    count = jnp.maximum(count, 1.0)
    for chunk in range(chunks):
        summed = jnp.dot(
            own, corrected[chunk].reshape(seg_dev * seg_rows, width), preferred_element_type=f32
        )
        for number in order:

            @pl.when(exists(along - SIDES[number], n_along))
            def _():
                slot_copy(chunk, number).wait_recv()

            summed = summed + jnp.dot(
                matrices[number],
                got_rows[chunk, number].reshape(CAP * seg_rows, width),
                preferred_element_type=f32,
            )
        result = (summed / count).reshape(rows, bands, width)
        out_ref[:, :, chunk * width : (chunk + 1) * width] = result.astype(bf16)
    for number, (da, dc) in enumerate(DIRECTIONS):

        @pl.when(both(along + da, n_along, across + dc, n_across))
        def _():
            halo_copy(number, da, dc).wait_send()

    for number in order:

        @pl.when(exists(along + SIDES[number], n_along))
        def _():
            tag_copy(number).wait_send()
            for chunk in range(chunks):
                slot_copy(chunk, number).wait_send()


def body(
    n_along,
    n_across,
    toa_bands,
    dark_mask,
    vapour,
    elev_class,
    elev_frac,
    kernel,
    lut_gain,
    lut_path,
    lut_albedo,
    routes,
    starts,
):
    rows, bands, cols = toa_bands.shape
    half = kernel.shape[0] // 2
    halo = -(-half // 16) * 16
    levels = lut_gain.shape[1:]
    levels_e, levels_a, levels_w = levels
    seg_dev = routes.shape[0]
    seg_rows = SEG * bands
    side_count = len(SIDES)
    width = math.gcd(cols, 256)
    chunks = cols // width
    vmem = pl.BlockSpec(memory_space=pltpu.VMEM)
    smem = pl.BlockSpec(memory_space=pltpu.SMEM)
    anywhere = pl.BlockSpec(memory_space=pl.ANY)
    dma = pltpu.SemaphoreType.DMA

    def table(lut):
        return lut.transpose(0, 1, 3, 2).reshape(bands * levels_e * levels_w, levels_a)

    flat, fields, tags = pl.pallas_call(
        prep_kernel,
        out_shape=(
            jax.ShapeDtypeStruct((rows * bands, cols), bf16),
            jax.ShapeDtypeStruct((2, rows, cols), bf16),
            jax.ShapeDtypeStruct((side_count, 8, CAP * seg_rows), f32),
        ),
        in_specs=[vmem, vmem, smem, smem],
        out_specs=(vmem, vmem, vmem),
        name="prep",
    )(toa_bands, dark_mask, routes.T, starts.T)

    out = pl.pallas_call(
        functools.partial(main_kernel, n_along, n_across, bands, levels),
        out_shape=jax.ShapeDtypeStruct((rows, bands, cols), bf16),
        in_specs=[smem, smem] + [vmem] * 6 + [anywhere] * 4,
        out_specs=vmem,
        scratch_shapes=[
            pltpu.VMEM((rows * bands, cols), bf16),
            pltpu.VMEM((rows, cols), f32),
            pltpu.VMEM((rows, cols), jnp.int32),
            pltpu.VMEM((rows, cols), f32),
            pltpu.VMEM((8, LANES), f32),
            pltpu.VMEM((2, rows + 2 * halo, cols + 2 * LANES), bf16),
            pltpu.VMEM((rows, cols), f32),
            pltpu.VMEM((levels_w, rows, cols), f32),
            pltpu.VMEM((rows, cols), f32),
            pltpu.VMEM((chunks, seg_dev, seg_rows, width), bf16),
            pltpu.VMEM((chunks, side_count * CAP, seg_rows, width), bf16),
            pltpu.VMEM((chunks, side_count, CAP, seg_rows, width), bf16),
            pltpu.VMEM((side_count, 8, CAP * seg_rows), f32),
            dma((4,)),
            dma((len(DIRECTIONS),)),
            dma((len(DIRECTIONS),)),
            dma((side_count,)),
            dma((side_count,)),
            dma((chunks, side_count)),
            dma((chunks, side_count)),
        ],
        compiler_params=pltpu.CompilerParams(collective_id=0, has_side_effects=True),
        name="main",
    )(
        routes.T,
        starts.T,
        fields,
        tags,
        kernel[None],
        table(lut_gain),
        table(lut_path),
        table(lut_albedo),
        flat,
        vapour,
        elev_class,
        elev_frac,
    )
    return out[None]


def solution(mesh):
    in_specs = (
        P(("groups", "along"), None, "across"),
        P(("groups", "along"), "across"),
        P(("groups", "along"), "across"),
        P(("groups", "along"), "across"),
        P(("groups", "along"), "across"),
        P(),
        P(),
        P(),
        P(),
        P(("groups", "along"), None),
        P(("groups", "along"), None),
    )
    out_specs = P(("groups", "along"), None, None, "across")
    run = functools.partial(body, mesh.shape["along"], mesh.shape["across"])
    return jax.shard_map(run, mesh=mesh, in_specs=in_specs, out_specs=out_specs, check_vma=False)
```

time: 119 us -> 35.8 us (0.30)
  Pallas kernels: 0 us -> 33.5 us
  starting transfers between devices: 30.5 us -> 0 us
  other arithmetic: 28.3 us -> 0 us
  local copies, waits for them, and re-layouts: 28.7 us -> 2.02 us
  waiting for transfers between devices: 18.5 us -> 0 us
  matrix products: 11.3 us -> 0 us
    pallas_call x0 -> x2, Pallas kernels: none -> 33.5 us  [the longest x1 31.4 us: body(): pl.pallas_call(functools.partial(main_kernel, n_along, n_across, bands, l...]
    ppermute x12 -> x0, starting transfers between devices: 30.5 us -> none  [the longest x8 20.8 us: from_behind(): lax.ppermute(value, axis, [(source, source + steps) for source in range(i...]
    ppermute x12 -> x0, waiting for transfers between devices: 18.5 us -> none  [the longest x8 16.9 us: from_behind(): lax.ppermute(value, axis, [(source, source + steps) for source in range(i...]
    reduce_sum x12 -> x0, other arithmetic: 11.4 us -> none  [the longest x4 9.71 us: correct_block(): coefficient = jnp.sum(node_values * weight_e[None, None], axis=2)]
    dot_general x22 -> x0, matrix products: 11.3 us -> none  [the longest x4 3.91 us: correct_block(): jnp.dot(lut_table, joint_weight, preferred_element_type=jnp.float32)]
    while x4 -> x0, local copies, waits for them, and re-layouts: 11 us -> none
    while x4 -> x0, other arithmetic: 4.29 us -> none
    broadcast_in_dim x9 -> x0, other arithmetic: 4.01 us -> none  [the longest x4 3.56 us: correct_block(): jnp.where(elev_ids == class_block[None], 1.0 - frac_block[None], 0.0)]
  transfers between devices with their start and end apart: 12 -> 0, of which waited for: 5 -> 0; matrix products, arithmetic and copies ran while one was open for 7% -> 0% of each run, Pallas kernels for 0% -> 0%
where the time goes in v2:
time: 35.8 us; the launch traced here: 35.6 us
  Pallas kernels  33.5 us (94%)
  local copies, waits for them, and re-layouts  2.02 us (6%)
    pallas_call x1, Pallas kernels, body(): pl.pallas_call(functools.partial(main_kernel, n_along, n_across, bands, l...  31.4 us
    pallas_call x1, Pallas kernels, body(): pl.pallas_call(prep_kernel, out_shape=(jax.ShapeDtypeStruct((rows * bands...  2.16 us
    unnamed x1, local copies, waits for them, and re-layouts  2.02 us

profile of v2, /device:TPU:0, one launch (start us, length us, event | category | flops | bytes accessed | tf_op | source)
XLA Modules:
  0.0 35.6 jit_solution(17755805228610827490)
XLA Ops:
  0.0 2.2 %prep.1 = (bf16[256,1024]{1,0:T(8,128)(2,1)}, bf16[2,64,1024]{2,1,0:T(8,128)(2,1)}, f32[4,8,128]{2,1,0:T(8,128)}) custom-call(bf16[64,4,1024]{2,1,0:T(4,128)(2,1)} %toa_ref.1, s32[64,1024]{1,0:T(8,128)} %mask_ref.1, s32[2,4]{1,0:T(2,128)} %bitcast.17, s32[2,4]{1,0:T(2,128)} %bitcast.19), custom_call_target="tpu_custom_call" | custom-call | tf_op jit(solution)/shard_map/prep/pallas_call | solution.py:447
  2.2 31.4 %main.1 = bf16[64,4,1024]{2,1,0:T(4,128)(2,1)} custom-call(s32[2,4]{1,0:T(2,128)} %bitcast.18, s32[2,4]{1,0:T(2,128)} %bitcast.20, bf16[2,64,1024]{2,1,0:T(8,128)(2,1)} %get-tuple-element.8.fields_ref, f32[4,8,128]{2,1,0:T(8,128)} %get-tuple-element.9.tags_ref, f32[1,61]{1,0:T(1,128)} %bitcast.21, bf16[256,16]{1,0:T(8,128)(2,1)} %bitcast.14, ...), custom_call_target="tpu_custom_call" | custom-call | tf_op jit(solution)/shard_map/main/pallas_call | solution.py:459
  33.5 2.0 %copy.13 = bf16[1,64,4,1024]{3,2,1,0:T(4,128)(2,1)} copy(bf16[1,64,4,1024]{3,2,1,0:T(4,128)(2,1)} %bitcast.13) | data formatting | bytes 1048576

commit v3 on v2

--- a/solution.py
+++ b/solution.py
@@ -12,6 +12,7 @@
 REACH = 2
 CAP = 2
 LANES = 128
+WIDTH = 256
 MESH_ID = pl.DeviceIdType.MESH
 SIDES = [side - REACH for side in range(REACH)] + [side + 1 for side in range(REACH)]
 DIRECTIONS = [(da, dc) for da in (-1, 0, 1) for dc in (-1, 0, 1) if (da, dc) != (0, 0)]
@@ -46,32 +47,6 @@
     return exists(position_a, count_a) & exists(position_c, count_c)
 
 
-def prep_kernel(toa_ref, mask_ref, routes_ref, starts_ref, flat_ref, fields_ref, tags_ref):
-    rows, bands, cols = toa_ref.shape
-    own = lax.axis_index("along")
-    flat = toa_ref[...].astype(f32).reshape(rows * bands, cols).astype(bf16)
-    flat_ref[...] = flat
-    row = lax.broadcasted_iota(jnp.int32, (rows, rows * bands), 0) * bands
-    col = lax.broadcasted_iota(jnp.int32, (rows, rows * bands), 1)
-    pick = jnp.where(col == row, 8.0, 0.0) + jnp.where(col == row + 2, -4.0, 0.0)
-    darkness = mask_ref[...].astype(f32)
-    value = jnp.dot(pick.astype(bf16), flat, preferred_element_type=f32)
-    fields_ref[0] = (darkness * value).astype(bf16)
-    fields_ref[1] = darkness.astype(bf16)
-    seg_rows = SEG * bands
-    lane = lax.broadcasted_iota(jnp.int32, (8, CAP * seg_rows), 1)
-    for number, side in enumerate(SIDES):
-        target = jnp.full((8, CAP * seg_rows), -1, jnp.int32)
-        rank = jnp.int32(0)
-        for s in range(routes_ref.shape[1]):
-            hit = routes_ref[1, s] - own == side
-            place = jnp.where(hit, rank, -1)
-            inside = (lane >= place * seg_rows) & (lane < (place + 1) * seg_rows) & (place >= 0)
-            target = jnp.where(inside, starts_ref[1, s] * bands + lane - place * seg_rows, target)
-            rank = rank + jnp.where(hit, 1, 0)
-        tags_ref[number] = target.astype(f32)
-
-
 def main_kernel(
     n_along,
     n_across,
@@ -79,23 +54,32 @@
     levels,
     routes_ref,
     starts_ref,
-    fields_ref,
-    tags_ref,
+    toa_hbm,
+    mask_hbm,
+    taps_hbm,
+    gain_hbm,
+    path_hbm,
+    albedo_hbm,
+    vapour_hbm,
+    class_hbm,
+    frac_hbm,
+    out_ref,
+    raw_ref,
+    mask_ref,
     taps_ref,
     gain_ref,
     path_ref,
     albedo_ref,
-    toa_hbm,
-    vapour_hbm,
-    class_hbm,
-    frac_hbm,
-    out_ref,
-    toa_ref,
     vapour_ref,
     class_ref,
     frac_ref,
+    toa_ref,
+    fields_ref,
+    tags_ref,
     taps_pad,
     padded,
+    tall_high,
+    tall_low,
     pos_ref,
     weights,
     heights,
@@ -113,21 +97,28 @@
 ):
     along, across = lax.axis_index("along"), lax.axis_index("across")
     levels_e, levels_a, levels_w = levels
-    rows, cols = fields_ref.shape[1], fields_ref.shape[2]
+    rows, _, cols = toa_hbm.shape
     halo = (padded.shape[1] - rows) // 2
-    half = taps_ref.shape[1] // 2
+    half = taps_hbm.shape[1] // 2
     chunks, seg_dev, seg_rows, width = corrected.shape
     loads = [
         pltpu.make_async_copy(source, target, load_sem.at[number])
         for number, (source, target) in enumerate(
             (
+                (toa_hbm, raw_ref),
+                (mask_hbm, mask_ref),
+                (taps_hbm, taps_ref),
+                (gain_hbm, gain_ref),
+                (path_hbm, path_ref),
+                (albedo_hbm, albedo_ref),
                 (vapour_hbm, vapour_ref),
                 (class_hbm, class_ref),
                 (frac_hbm, frac_ref),
-                (toa_hbm, toa_ref),
             )
         )
     ]
+    for load in loads:
+        load.start()
     barrier = pltpu.get_barrier_semaphore()
     peers = DIRECTIONS + [(side, 0) for side in SIDES if (side, 0) not in DIRECTIONS]
     for da, dc in peers:
@@ -141,8 +132,28 @@
                 device_id_type=MESH_ID,
             )
 
-    for load in loads:
-        load.start()
+    for load in loads[:2]:
+        load.wait()
+    flat = raw_ref[...].astype(f32).reshape(rows * bands, cols).astype(bf16)
+    row = lax.broadcasted_iota(jnp.int32, (rows, rows * bands), 0) * bands
+    col = lax.broadcasted_iota(jnp.int32, (rows, rows * bands), 1)
+    pick = jnp.where(col == row, 8.0, 0.0) + jnp.where(col == row + 2, -4.0, 0.0)
+    darkness = mask_ref[...].astype(f32)
+    value = jnp.dot(pick.astype(bf16), flat, preferred_element_type=f32)
+    fields_ref[0] = (darkness * value).astype(bf16)
+    fields_ref[1] = darkness.astype(bf16)
+    padded[:, halo : halo + rows, LANES : LANES + cols] = fields_ref[...]
+    lane = lax.broadcasted_iota(jnp.int32, (8, CAP * seg_rows), 1)
+    for number, side in enumerate(SIDES):
+        target = jnp.full((8, CAP * seg_rows), -1, jnp.int32)
+        rank = jnp.int32(0)
+        for s in range(seg_dev):
+            hit = routes_ref[1, s] - along == side
+            place = jnp.where(hit, rank, -1)
+            inside = (lane >= place * seg_rows) & (lane < (place + 1) * seg_rows) & (place >= 0)
+            target = jnp.where(inside, starts_ref[1, s] * bands + lane - place * seg_rows, target)
+            rank = rank + jnp.where(hit, 1, 0)
+        tags_ref[number] = target.astype(f32)
     spans = {
         -1: (slice(0, halo), slice(halo + rows, 2 * halo + rows)),
         0: (slice(0, rows), slice(halo, halo + rows)),
@@ -154,10 +165,25 @@
         1: (slice(cols - LANES, cols), slice(0, LANES)),
     }
 
-    def halo_copy(number, da, dc):
+    copies = []
+    for da, dc in DIRECTIONS:
+        if dc:
+            copies.append((da, dc, lanes[dc][0], lanes[dc][1], 0 if dc > 0 else chunks - 1))
+    begin = 0
+    for chunk in range(chunks):
+        end = min(cols, (chunk + 1) * width + LANES)
+        if end > begin:
+            for da in (-1, 1):
+                copies.append(
+                    (da, 0, slice(begin, end), slice(LANES + begin, LANES + end), chunk)
+                )
+        begin = end
+
+    def halo_copy(number):
+        da, dc, source, target, _ = copies[number]
         return pltpu.make_async_remote_copy(
-            src_ref=fields_ref.at[:, spans[da][0], lanes[dc][0]],
-            dst_ref=padded.at[:, spans[da][1], lanes[dc][1]],
+            src_ref=fields_ref.at[:, spans[da][0], source],
+            dst_ref=padded.at[:, spans[da][1], target],
             send_sem=halo_send.at[number],
             recv_sem=halo_recv.at[number],
             device_id={"along": along + da, "across": across + dc},
@@ -190,11 +216,11 @@
             both(along + da, n_along, across + dc, n_across).astype(jnp.int32) for da, dc in peers
         ),
     )
-    for number, (da, dc) in enumerate(DIRECTIONS):
+    for number, (da, dc, _, _, _) in enumerate(copies):
 
         @pl.when(both(along + da, n_along, across + dc, n_across))
         def _():
-            halo_copy(number, da, dc).start()
+            halo_copy(number).start()
 
     order = sorted(range(len(SIDES)), key=lambda number: abs(SIDES[number]))
     for number in order:
@@ -208,7 +234,7 @@
             got_rows[:, number] = jnp.zeros((chunks, CAP, seg_rows, width), bf16)
             got_tags[number] = jnp.full(got_tags.shape[1:], -1.0, f32)
 
-    padded[:, spans[0][1], lanes[0][1]] = fields_ref[...]
+    toa_ref[...] = flat
     for da, dc in DIRECTIONS:
 
         @pl.when(jnp.logical_not(both(along - da, n_along, across - dc, n_across)))
@@ -216,6 +242,8 @@
             target = padded.at[:, spans[da][1], lanes[dc][1]]
             target[...] = jnp.zeros(target.shape, bf16)
 
+    for load in loads[2:6]:
+        load.wait()
     taps_pad[...] = jnp.zeros(taps_pad.shape, f32)
     taps_pad[0:1, 0 : taps_ref.shape[1]] = taps_ref[...]
     taps = taps_pad[0:1, :]
@@ -242,32 +270,32 @@
         jnp.where(source == wanted, 1.0, 0.0).astype(bf16), wide, preferred_element_type=f32
     ).astype(bf16)
 
-    for load in loads:
+    for load in loads[6:]:
         load.wait()
     for w in range(levels_w):
         weights[w] = jnp.maximum(0.0, 1.0 - jnp.abs(vapour_ref[...] - float(w)))
     heights[...] = class_ref[...].astype(f32) + frac_ref[...]
 
-    for number, (da, dc) in enumerate(DIRECTIONS):
-
-        @pl.when(both(along - da, n_along, across - dc, n_across))
-        def _():
-            halo_copy(number, da, dc).wait_recv()
-
-    tall = []
-    for field in range(2):
-        product = jnp.dot(down, padded[field], preferred_element_type=f32)
-        tall.append(product[:rows] + product[rows:])
-    tall_high, tall_low = split(jnp.concatenate(tall, axis=0))
-    for number in range(chunks):
-        window = slice(number * block, number * block + block + 2 * LANES)
+    def smooth(chunk):
+        for number, (da, dc, _, _, needed) in enumerate(copies):
+            if needed == chunk:
+
+                @pl.when(both(along - da, n_along, across - dc, n_across))
+                def _():
+                    halo_copy(number).wait_recv()
+
+        fresh = slice(chunk * width + 2 * LANES if chunk else 0, (chunk + 1) * width + 2 * LANES)
+        for field in range(2):
+            product = jnp.dot(down, padded[field, :, fresh], preferred_element_type=f32)
+            high, low = split(product[:rows] + product[rows:])
+            tall_high[field * rows : (field + 1) * rows, fresh] = high
+            tall_low[field * rows : (field + 1) * rows, fresh] = low
+        window = slice(chunk * width, chunk * width + width + 2 * LANES)
         smoothed = dot_nt(tall_high[:, window], across_high)
         smoothed += dot_nt(tall_low[:, window], across_high)
         smoothed += dot_nt(tall_high[:, window], across_low)
         aerosol = smoothed[:rows] / jnp.maximum(smoothed[rows:], 1.0)
-        pos_ref[:, number * block : (number + 1) * block] = (levels_a - 1) * jax.nn.sigmoid(
-            aerosol
-        )
+        pos_ref[:, chunk * width : (chunk + 1) * width] = (levels_a - 1) * jax.nn.sigmoid(aerosol)
 
     chosen = []
     for number, side in enumerate(SIDES):
@@ -286,6 +314,7 @@
     pair_e = (sub // bands).astype(f32)
     per_tile = 8 // bands
     quad = 16 // bands
+    group = max(1, 256 // width)
 
     def correct(chunk, seg):
         at_cols = slice(chunk * width, (chunk + 1) * width)
@@ -295,16 +324,26 @@
         height_rows = heights[pl.ds(base, SEG), at_cols]
         for first in range(0, SEG, quad):
             partial = []
+            values = []
+            for start in range(first, first + quad, group):
+                joints = []
+                for row in range(start, start + group):
+                    weight_a = jnp.maximum(0.0, 1.0 - jnp.abs(position[row : row + 1] - node_a))
+                    joints.append(
+                        jnp.concatenate(
+                            [
+                                (weight_a * weights[w, pl.ds(base + row, 1), at_cols]).astype(bf16)
+                                for w in range(levels_w)
+                            ],
+                            axis=0,
+                        )
+                    )
+                joint = joints[0] if group == 1 else jnp.concatenate(joints, axis=1)
+                product = jnp.dot(lut, joint, preferred_element_type=f32)
+                for k in range(group):
+                    values.append(product[:, k * width : (k + 1) * width])
             for row in range(first, first + quad):
-                weight_a = jnp.maximum(0.0, 1.0 - jnp.abs(position[row : row + 1] - node_a))
-                joint = jnp.concatenate(
-                    [
-                        (weight_a * weights[w, pl.ds(base + row, 1), at_cols]).astype(bf16)
-                        for w in range(levels_w)
-                    ],
-                    axis=0,
-                )
-                nodes = jnp.dot(lut, joint, preferred_element_type=f32)
+                nodes = values[row - first]
                 height = height_rows[row : row + 1]
                 sums = [None] * 3
                 for k in range(table_rows // 8):
@@ -350,10 +389,10 @@
         return jnp.where(row == target, 1.0, 0.0)
 
     for chunk in range(chunks):
-        correct_from(chunk, 0, 1)
+        smooth(chunk)
         if chunk:
             start_slots(chunk - 1)
-        correct_from(chunk, 1, seg_dev)
+        correct_from(chunk, 0, seg_dev)
         for number in range(len(SIDES)):
             for k in range(CAP):
                 slots[chunk, number * CAP + k] = corrected[chunk, chosen[number][k]]
@@ -396,11 +435,11 @@
             )
         result = (summed / count).reshape(rows, bands, width)
         out_ref[:, :, chunk * width : (chunk + 1) * width] = result.astype(bf16)
-    for number, (da, dc) in enumerate(DIRECTIONS):
+    for number, (da, dc, _, _, _) in enumerate(copies):
 
         @pl.when(both(along + da, n_along, across + dc, n_across))
         def _():
-            halo_copy(number, da, dc).wait_send()
+            halo_copy(number).wait_send()
 
     for number in order:
 
@@ -434,40 +473,39 @@
     seg_dev = routes.shape[0]
     seg_rows = SEG * bands
     side_count = len(SIDES)
-    width = math.gcd(cols, 256)
+    width = math.gcd(cols, WIDTH)
     chunks = cols // width
     vmem = pl.BlockSpec(memory_space=pltpu.VMEM)
     smem = pl.BlockSpec(memory_space=pltpu.SMEM)
-    anywhere = pl.BlockSpec(memory_space=pl.ANY)
+    hbm = pl.BlockSpec(memory_space=pltpu.HBM)
+    table_shape = (bands * levels_e * levels_w, levels_a)
     dma = pltpu.SemaphoreType.DMA
 
     def table(lut):
-        return lut.transpose(0, 1, 3, 2).reshape(bands * levels_e * levels_w, levels_a)
-
-    flat, fields, tags = pl.pallas_call(
-        prep_kernel,
-        out_shape=(
-            jax.ShapeDtypeStruct((rows * bands, cols), bf16),
-            jax.ShapeDtypeStruct((2, rows, cols), bf16),
-            jax.ShapeDtypeStruct((side_count, 8, CAP * seg_rows), f32),
-        ),
-        in_specs=[vmem, vmem, smem, smem],
-        out_specs=(vmem, vmem, vmem),
-        name="prep",
-    )(toa_bands, dark_mask, routes.T, starts.T)
+        return lut.transpose(0, 1, 3, 2).reshape(table_shape)
 
     out = pl.pallas_call(
         functools.partial(main_kernel, n_along, n_across, bands, levels),
         out_shape=jax.ShapeDtypeStruct((rows, bands, cols), bf16),
-        in_specs=[smem, smem] + [vmem] * 6 + [anywhere] * 4,
+        in_specs=[smem, smem] + [hbm] * 9,
         out_specs=vmem,
         scratch_shapes=[
-            pltpu.VMEM((rows * bands, cols), bf16),
+            pltpu.VMEM((rows, bands, cols), bf16),
+            pltpu.VMEM((rows, cols), jnp.int32),
+            pltpu.VMEM((1, kernel.shape[0]), f32),
+            pltpu.VMEM(table_shape, bf16),
+            pltpu.VMEM(table_shape, bf16),
+            pltpu.VMEM(table_shape, bf16),
             pltpu.VMEM((rows, cols), f32),
             pltpu.VMEM((rows, cols), jnp.int32),
             pltpu.VMEM((rows, cols), f32),
+            pltpu.VMEM((rows * bands, cols), bf16),
+            pltpu.VMEM((2, rows, cols), bf16),
+            pltpu.VMEM((side_count, 8, CAP * seg_rows), f32),
             pltpu.VMEM((8, LANES), f32),
             pltpu.VMEM((2, rows + 2 * halo, cols + 2 * LANES), bf16),
+            pltpu.VMEM((2 * rows, cols + 2 * LANES), bf16),
+            pltpu.VMEM((2 * rows, cols + 2 * LANES), bf16),
             pltpu.VMEM((rows, cols), f32),
             pltpu.VMEM((levels_w, rows, cols), f32),
             pltpu.VMEM((rows, cols), f32),
@@ -475,29 +513,35 @@
             pltpu.VMEM((chunks, side_count * CAP, seg_rows, width), bf16),
             pltpu.VMEM((chunks, side_count, CAP, seg_rows, width), bf16),
             pltpu.VMEM((side_count, 8, CAP * seg_rows), f32),
-            dma((4,)),
-            dma((len(DIRECTIONS),)),
-            dma((len(DIRECTIONS),)),
+            dma((9,)),
+            dma((6 + 2 * chunks,)),
+            dma((6 + 2 * chunks,)),
             dma((side_count,)),
             dma((side_count,)),
             dma((chunks, side_count)),
             dma((chunks, side_count)),
         ],
-        compiler_params=pltpu.CompilerParams(collective_id=0, has_side_effects=True),
+        compiler_params=pltpu.CompilerParams(
+            collective_id=0, has_side_effects=True, vmem_limit_bytes=28 * 1024 * 1024
+        ),
         name="main",
     )(
         routes.T,
         starts.T,
-        fields,
-        tags,
-        kernel[None],
-        table(lut_gain),
-        table(lut_path),
-        table(lut_albedo),
-        flat,
-        vapour,
-        elev_class,
-        elev_frac,
+        *(
+            pltpu.with_memory_space_constraint(value, pltpu.HBM)
+            for value in (
+                toa_bands,
+                dark_mask,
+                kernel[None],
+                table(lut_gain),
+                table(lut_path),
+                table(lut_albedo),
+                vapour,
+                elev_class,
+                elev_frac,
+            )
+        ),
     )
     return out[None]
 

time: 35.8 us -> 29.7 us (0.83)
  Pallas kernels: 33.5 us -> 28.1 us
  local copies, waits for them, and re-layouts: 2.02 us -> 1.49 us
    pallas_call x1, Pallas kernels: 31.4 us -> 28.1 us  [body(): pl.pallas_call(functools.partial(main_kernel, n_along, n_across, bands, l...]
    pallas_call x1 -> x0, Pallas kernels: 2.16 us -> none  [body(): pl.pallas_call(prep_kernel, out_shape=(jax.ShapeDtypeStruct((rows * bands...]
    unnamed x1 -> x5, local copies, waits for them, and re-layouts: 2.02 us -> 1.49 us
where the time goes in v3:
time: 29.7 us; the launch traced here: 29.6 us
  Pallas kernels  28.1 us (95%)
  local copies, waits for them, and re-layouts  1.49 us (5%)
    pallas_call x1, Pallas kernels, body(): pl.pallas_call(functools.partial(main_kernel, n_along, n_across, bands, l...  28.1 us
    unnamed x5, local copies, waits for them, and re-layouts  1.49 us

profile of v3, /device:TPU:0, one launch (start us, length us, event | category | flops | bytes accessed | tf_op | source)
XLA Modules:
  0.0 29.6 jit_solution(2247132524978564189)
XLA Ops:
  0.0 0.0 copy-start.1
  0.0 0.0 copy-start
  0.0 0.7 %copy-done.1 = s32[4,2]{0,1:T(2,128)S(1)} copy-done((s32[4,2]{0,1:T(2,128)S(1)}, s32[4,2]{0,1:T(2,128)}, u32[]{:S(2)}) %copy-start.1) | copy-done | bytes 56
  0.7 0.0 copy-done
  0.7 28.1 %main.1 = bf16[64,4,1024]{2,1,0:T(4,128)(2,1)S(1)} custom-call(s32[2,4]{1,0:T(2,128)S(1)} %bitcast.14, s32[2,4]{1,0:T(2,128)S(1)} %bitcast.15, bf16[64,4,1024]{2,1,0:T(4,128)(2,1)} %toa_hbm.1, s32[64,1024]{1,0:T(8,128)} %mask_hbm.1, f32[1,61]{1,0:T(1,128)} %bitcast.19, bf16[256,16]{1,0:T(8,128)(2,1)} %bitcast.16, bf16[256,16]{1,0:T(8,128)(2,1)} %bitcast.17, ...), custom_call_target="tpu_custom_call" | custom-call | tf_op jit(solution)/shard_map/main/pallas_call | solution.py:487
  28.8 0.8 %copy.13 = bf16[1,64,4,1024]{3,2,1,0:T(4,128)(2,1)} copy(bf16[1,64,4,1024]{3,2,1,0:T(4,128)(2,1)S(1)} %bitcast.13) | data formatting | bytes 1048576
Async XLA Ops:
  0.0 0.7 %copy-start.1 = (s32[4,2]{0,1:T(2,128)S(1)}, s32[4,2]{0,1:T(2,128)}, u32[]{:S(2)}) copy-start(s32[4,2]{0,1:T(2,128)} %param.21) | copy-start | bytes 100
  0.0 0.7 %copy-start = (s32[4,2]{0,1:T(2,128)S(1)}, s32[4,2]{0,1:T(2,128)}, u32[]{:S(2)}) copy-start(s32[4,2]{0,1:T(2,128)} %param.20) | copy-start | bytes 100

commit v4 on v3

--- a/solution.py
+++ b/solution.py
@@ -12,7 +12,7 @@
 REACH = 2
 CAP = 2
 LANES = 128
-WIDTH = 256
+WIDTH = 128
 MESH_ID = pl.DeviceIdType.MESH
 SIDES = [side - REACH for side in range(REACH)] + [side + 1 for side in range(REACH)]
 DIRECTIONS = [(da, dc) for da in (-1, 0, 1) for dc in (-1, 0, 1) if (da, dc) != (0, 0)]
@@ -52,8 +52,8 @@
     n_across,
     bands,
     levels,
-    routes_ref,
-    starts_ref,
+    routes_hbm,
+    starts_hbm,
     toa_hbm,
     mask_hbm,
     taps_hbm,
@@ -64,6 +64,8 @@
     class_hbm,
     frac_hbm,
     out_ref,
+    routes_ref,
+    starts_ref,
     raw_ref,
     mask_ref,
     taps_ref,
@@ -114,6 +116,8 @@
                 (vapour_hbm, vapour_ref),
                 (class_hbm, class_ref),
                 (frac_hbm, frac_ref),
+                (routes_hbm, routes_ref),
+                (starts_hbm, starts_ref),
             )
         )
     ]
@@ -143,6 +147,8 @@
     fields_ref[0] = (darkness * value).astype(bf16)
     fields_ref[1] = darkness.astype(bf16)
     padded[:, halo : halo + rows, LANES : LANES + cols] = fields_ref[...]
+    for load in loads[9:]:
+        load.wait()
     lane = lax.broadcasted_iota(jnp.int32, (8, CAP * seg_rows), 1)
     for number, side in enumerate(SIDES):
         target = jnp.full((8, CAP * seg_rows), -1, jnp.int32)
@@ -270,10 +276,11 @@
         jnp.where(source == wanted, 1.0, 0.0).astype(bf16), wide, preferred_element_type=f32
     ).astype(bf16)
 
-    for load in loads[6:]:
+    for load in loads[6:9]:
         load.wait()
     for w in range(levels_w):
-        weights[w] = jnp.maximum(0.0, 1.0 - jnp.abs(vapour_ref[...] - float(w)))
+        weight_w = jnp.maximum(0.0, 1.0 - jnp.abs(vapour_ref[...] - float(w)))
+        weights[w] = weight_w.reshape(seg_dev, SEG, cols)
     heights[...] = class_ref[...].astype(f32) + frac_ref[...]
 
     def smooth(chunk):
@@ -332,7 +339,7 @@
                     joints.append(
                         jnp.concatenate(
                             [
-                                (weight_a * weights[w, pl.ds(base + row, 1), at_cols]).astype(bf16)
+                                (weight_a * weights[w, seg, row : row + 1, at_cols]).astype(bf16)
                                 for w in range(levels_w)
                             ],
                             axis=0,
@@ -476,7 +483,6 @@
     width = math.gcd(cols, WIDTH)
     chunks = cols // width
     vmem = pl.BlockSpec(memory_space=pltpu.VMEM)
-    smem = pl.BlockSpec(memory_space=pltpu.SMEM)
     hbm = pl.BlockSpec(memory_space=pltpu.HBM)
     table_shape = (bands * levels_e * levels_w, levels_a)
     dma = pltpu.SemaphoreType.DMA
@@ -487,9 +493,11 @@
     out = pl.pallas_call(
         functools.partial(main_kernel, n_along, n_across, bands, levels),
         out_shape=jax.ShapeDtypeStruct((rows, bands, cols), bf16),
-        in_specs=[smem, smem] + [hbm] * 9,
+        in_specs=[hbm] * 11,
         out_specs=vmem,
         scratch_shapes=[
+            pltpu.SMEM((2, seg_dev), jnp.int32),
+            pltpu.SMEM((2, seg_dev), jnp.int32),
             pltpu.VMEM((rows, bands, cols), bf16),
             pltpu.VMEM((rows, cols), jnp.int32),
             pltpu.VMEM((1, kernel.shape[0]), f32),
@@ -507,13 +515,13 @@
             pltpu.VMEM((2 * rows, cols + 2 * LANES), bf16),
             pltpu.VMEM((2 * rows, cols + 2 * LANES), bf16),
             pltpu.VMEM((rows, cols), f32),
-            pltpu.VMEM((levels_w, rows, cols), f32),
+            pltpu.VMEM((levels_w, seg_dev, SEG, cols), f32),
             pltpu.VMEM((rows, cols), f32),
             pltpu.VMEM((chunks, seg_dev, seg_rows, width), bf16),
             pltpu.VMEM((chunks, side_count * CAP, seg_rows, width), bf16),
             pltpu.VMEM((chunks, side_count, CAP, seg_rows, width), bf16),
             pltpu.VMEM((side_count, 8, CAP * seg_rows), f32),
-            dma((9,)),
+            dma((11,)),
             dma((6 + 2 * chunks,)),
             dma((6 + 2 * chunks,)),
             dma((side_count,)),
@@ -526,11 +534,11 @@
         ),
         name="main",
     )(
-        routes.T,
-        starts.T,
         *(
             pltpu.with_memory_space_constraint(value, pltpu.HBM)
             for value in (
+                routes.T,
+                starts.T,
                 toa_bands,
                 dark_mask,
                 kernel[None],

time: 29.7 us -> 28.6 us (0.963)
  local copies, waits for them, and re-layouts: 1.49 us -> 0.8 us
  Pallas kernels: 28.1 us -> 27.6 us
    unnamed x5 -> x1, local copies, waits for them, and re-layouts: 1.49 us -> 0.8 us
    pallas_call x1, Pallas kernels: 28.1 us -> 27.6 us  [body(): pl.pallas_call(functools.partial(main_kernel, n_along, n_across, bands, l...]
where the time goes in v4:
time: 28.6 us; the launch traced here: 28.4 us
  Pallas kernels  27.6 us (97%)
  local copies, waits for them, and re-layouts  0.8 us (3%)
    pallas_call x1, Pallas kernels, body(): pl.pallas_call(functools.partial(main_kernel, n_along, n_across, bands, l...  27.6 us
    unnamed x1, local copies, waits for them, and re-layouts  0.8 us

profile of v4, /device:TPU:0, one launch (start us, length us, event | category | flops | bytes accessed | tf_op | source)
XLA Modules:
  0.0 28.4 jit_solution(13522968227057281007)
XLA Ops:
  0.0 27.6 %main.1 = bf16[64,4,1024]{2,1,0:T(4,128)(2,1)S(1)} custom-call(s32[2,4]{1,0:T(2,128)} %bitcast.17, s32[2,4]{1,0:T(2,128)} %bitcast.18, bf16[64,4,1024]{2,1,0:T(4,128)(2,1)} %toa_hbm.1, s32[64,1024]{1,0:T(8,128)} %mask_hbm.1, f32[1,61]{1,0:T(1,128)} %bitcast.19, bf16[256,16]{1,0:T(8,128)(2,1)} %bitcast.14, bf16[256,16]{1,0:T(8,128)(2,1)} %bitcast.15, ...), custom_call_target="tpu_custom_call" | custom-call | tf_op jit(solution)/shard_map/main/pallas_call | solution.py:493
  27.6 0.8 %copy.13 = bf16[1,64,4,1024]{3,2,1,0:T(4,128)(2,1)} copy(bf16[1,64,4,1024]{3,2,1,0:T(4,128)(2,1)S(1)} %bitcast.13) | data formatting | bytes 1048576

commit v5 on v4

--- a/solution.py
+++ b/solution.py
@@ -121,7 +121,7 @@
             )
         )
     ]
-    for load in loads:
+    for load in loads[:2]:
         load.start()
     barrier = pltpu.get_barrier_semaphore()
     peers = DIRECTIONS + [(side, 0) for side in SIDES if (side, 0) not in DIRECTIONS]
@@ -136,16 +136,86 @@
                 device_id_type=MESH_ID,
             )
 
-    for load in loads[:2]:
-        load.wait()
-    flat = raw_ref[...].astype(f32).reshape(rows * bands, cols).astype(bf16)
     row = lax.broadcasted_iota(jnp.int32, (rows, rows * bands), 0) * bands
     col = lax.broadcasted_iota(jnp.int32, (rows, rows * bands), 1)
     pick = jnp.where(col == row, 8.0, 0.0) + jnp.where(col == row + 2, -4.0, 0.0)
+    for load in loads[:2]:
+        load.wait()
+    for load in loads[2:]:
+        load.start()
+    flat = raw_ref[...].astype(f32).reshape(rows * bands, cols).astype(bf16)
     darkness = mask_ref[...].astype(f32)
     value = jnp.dot(pick.astype(bf16), flat, preferred_element_type=f32)
     fields_ref[0] = (darkness * value).astype(bf16)
     fields_ref[1] = darkness.astype(bf16)
+    spans = {
+        -1: (slice(0, halo), slice(halo + rows, 2 * halo + rows)),
+        0: (slice(0, rows), slice(halo, halo + rows)),
+        1: (slice(rows - halo, rows), slice(0, halo)),
+    }
+    lanes = {
+        -1: (slice(0, LANES), slice(LANES + cols, 2 * LANES + cols)),
+        0: (slice(0, cols), slice(LANES, LANES + cols)),
+        1: (slice(cols - LANES, cols), slice(0, LANES)),
+    }
+
+    copies = []
+    for da, dc in DIRECTIONS:
+        if dc:
+            copies.append((da, dc, lanes[dc][0], lanes[dc][1], 0 if dc > 0 else chunks - 1))
+    begin = 0
+    for chunk in range(chunks):
+        end = min(cols, (chunk + 1) * width + LANES)
+        if end > begin:
+            for da in (-1, 1):
+                copies.append(
+                    (da, 0, slice(begin, end), slice(LANES + begin, LANES + end), chunk)
+                )
+        begin = end
+
+    def halo_copy(number):
+        da, dc, source, target, _ = copies[number]
+        return pltpu.make_async_remote_copy(
+            src_ref=fields_ref.at[:, spans[da][0], source],
+            dst_ref=padded.at[:, spans[da][1], target],
+            send_sem=halo_send.at[number],
+            recv_sem=halo_recv.at[number],
+            device_id={"along": along + da, "across": across + dc},
+            device_id_type=MESH_ID,
+        )
+
+    def tag_copy(number):
+        return pltpu.make_async_remote_copy(
+            src_ref=tags_ref.at[number],
+            dst_ref=got_tags.at[number],
+            send_sem=tag_send.at[number],
+            recv_sem=tag_recv.at[number],
+            device_id={"along": along + SIDES[number]},
+            device_id_type=MESH_ID,
+        )
+
+    def slot_copy(chunk, number):
+        return pltpu.make_async_remote_copy(
+            src_ref=slots.at[chunk, pl.ds(number * CAP, CAP)],
+            dst_ref=got_rows.at[chunk, number],
+            send_sem=slot_send.at[chunk, number],
+            recv_sem=slot_recv.at[chunk, number],
+            device_id={"along": along + SIDES[number]},
+            device_id_type=MESH_ID,
+        )
+
+    pl.semaphore_wait(
+        barrier,
+        sum(
+            both(along + da, n_along, across + dc, n_across).astype(jnp.int32) for da, dc in peers
+        ),
+    )
+    for number, (da, dc, _, _, _) in enumerate(copies):
+
+        @pl.when(both(along + da, n_along, across + dc, n_across))
+        def _():
+            halo_copy(number).start()
+
     padded[:, halo : halo + rows, LANES : LANES + cols] = fields_ref[...]
     for load in loads[9:]:
         load.wait()
@@ -160,74 +230,6 @@
             target = jnp.where(inside, starts_ref[1, s] * bands + lane - place * seg_rows, target)
             rank = rank + jnp.where(hit, 1, 0)
         tags_ref[number] = target.astype(f32)
-    spans = {
-        -1: (slice(0, halo), slice(halo + rows, 2 * halo + rows)),
-        0: (slice(0, rows), slice(halo, halo + rows)),
-        1: (slice(rows - halo, rows), slice(0, halo)),
-    }
-    lanes = {
-        -1: (slice(0, LANES), slice(LANES + cols, 2 * LANES + cols)),
-        0: (slice(0, cols), slice(LANES, LANES + cols)),
-        1: (slice(cols - LANES, cols), slice(0, LANES)),
-    }
-
-    copies = []
-    for da, dc in DIRECTIONS:
-        if dc:
-            copies.append((da, dc, lanes[dc][0], lanes[dc][1], 0 if dc > 0 else chunks - 1))
-    begin = 0
-    for chunk in range(chunks):
-        end = min(cols, (chunk + 1) * width + LANES)
-        if end > begin:
-            for da in (-1, 1):
-                copies.append(
-                    (da, 0, slice(begin, end), slice(LANES + begin, LANES + end), chunk)
-                )
-        begin = end
-
-    def halo_copy(number):
-        da, dc, source, target, _ = copies[number]
-        return pltpu.make_async_remote_copy(
-            src_ref=fields_ref.at[:, spans[da][0], source],
-            dst_ref=padded.at[:, spans[da][1], target],
-            send_sem=halo_send.at[number],
-            recv_sem=halo_recv.at[number],
-            device_id={"along": along + da, "across": across + dc},
-            device_id_type=MESH_ID,
-        )
-
-    def tag_copy(number):
-        return pltpu.make_async_remote_copy(
-            src_ref=tags_ref.at[number],
-            dst_ref=got_tags.at[number],
-            send_sem=tag_send.at[number],
-            recv_sem=tag_recv.at[number],
-            device_id={"along": along + SIDES[number]},
-            device_id_type=MESH_ID,
-        )
-
-    def slot_copy(chunk, number):
-        return pltpu.make_async_remote_copy(
-            src_ref=slots.at[chunk, pl.ds(number * CAP, CAP)],
-            dst_ref=got_rows.at[chunk, number],
-            send_sem=slot_send.at[chunk, number],
-            recv_sem=slot_recv.at[chunk, number],
-            device_id={"along": along + SIDES[number]},
-            device_id_type=MESH_ID,
-        )
-
-    pl.semaphore_wait(
-        barrier,
-        sum(
-            both(along + da, n_along, across + dc, n_across).astype(jnp.int32) for da, dc in peers
-        ),
-    )
-    for number, (da, dc, _, _, _) in enumerate(copies):
-
-        @pl.when(both(along + da, n_along, across + dc, n_across))
-        def _():
-            halo_copy(number).start()
-
     order = sorted(range(len(SIDES)), key=lambda number: abs(SIDES[number]))
     for number in order:
 

time: 28.6 us -> 28.5 us (level)
  no operation moved by 1% of the time
where the time goes in v5:
time: 28.5 us; the launch traced here: 28.3 us
  Pallas kernels  27.5 us (96%)
  local copies, waits for them, and re-layouts  0.8 us (3%)
    pallas_call x1, Pallas kernels, body(): pl.pallas_call(functools.partial(main_kernel, n_along, n_across, bands, l...  27.5 us
    unnamed x1, local copies, waits for them, and re-layouts  0.8 us

profile of v5, /device:TPU:0, one launch (start us, length us, event | category | flops | bytes accessed | tf_op | source)
XLA Modules:
  0.0 28.3 jit_solution(8233252626888167077)
XLA Ops:
  0.0 27.5 %main.1 = bf16[64,4,1024]{2,1,0:T(4,128)(2,1)S(1)} custom-call(s32[2,4]{1,0:T(2,128)} %bitcast.17, s32[2,4]{1,0:T(2,128)} %bitcast.18, bf16[64,4,1024]{2,1,0:T(4,128)(2,1)} %toa_hbm.1, s32[64,1024]{1,0:T(8,128)} %mask_hbm.1, f32[1,61]{1,0:T(1,128)} %bitcast.19, bf16[256,16]{1,0:T(8,128)(2,1)} %bitcast.14, bf16[256,16]{1,0:T(8,128)(2,1)} %bitcast.15, ...), custom_call_target="tpu_custom_call" | custom-call | tf_op jit(solution)/shard_map/main/pallas_call | solution.py:495
  27.5 0.8 %copy.13 = bf16[1,64,4,1024]{3,2,1,0:T(4,128)(2,1)} copy(bf16[1,64,4,1024]{3,2,1,0:T(4,128)(2,1)S(1)} %bitcast.13) | data formatting | bytes 1048576
